TPU v7x, 32 devices: a whole 2x2x4 slice. The times are simulated.
32 devices in a mesh: tensor: 8 (over z, core), example: 4 (over y, x).
Axes of the slice: x: 2, y: 2, z: 4, core: 2. Of those that a mesh axis runs over, the one named last changes fastest.
Arguments:
- acts: bfloat16 [256, 8192], P(None, 'example'), may hold values from -6 to 6
- out_grad: bfloat16 [256, 8192], P(None, 'example'), may hold values from -6 to 6
- w_gate: bfloat16 [8192, 28672], P('example', 'tensor'), may hold values from -0.0625 to 0.0625
- w_up: bfloat16 [8192, 28672], P('example', 'tensor'), may hold values from -0.0625 to 0.0625
- w_down: bfloat16 [28672, 8192], P('tensor', 'example'), may hold values from -0.03125 to 0.03125
- proj_in: bfloat16 [8192, 64], P('example'), may hold values from -0.0625 to 0.0625
- proj_gate: bfloat16 [28672, 64], P('tensor'), may hold values from -0.03125 to 0.03125
- proj_up: bfloat16 [28672, 64], P('tensor'), may hold values from -0.03125 to 0.03125
- proj_hidden: bfloat16 [28672, 64], P('tensor'), may hold values from -0.03125 to 0.03125
- proj_out: bfloat16 [8192, 64], P('example'), may hold values from -0.0625 to 0.0625
- store: bfloat16 [4096, 12288], P(('tensor', 'example')), may hold values from -0.0546875 to 0.0546875
- doc_ids: int32 [32, 128], P(('tensor', 'example')), may hold values from 0 to 127, each once within a row
Outputs:
- scores: float32 [4, 4096], P(None, ('tensor', 'example'))
Inputs may be any that keep to these rules, and one draw needn't show every extreme that they name: Each row of doc_ids is a permutation of 0 to 127.
All inputs are finite; a program needn't handle non-finite values.
Results may differ from a plain program's by a relative error of at most 0.022.
Values may be sent and summed in bfloat16 or wider, within the bound.
No kernel may reach another device: no remote copies, remote signals or barrier semaphores. Data moves between devices by JAX's collectives and lax.ppermute only.
A program may use at most 128 MiB of HBM per device.

v0:
```python
import jax
import jax.numpy as jnp
from jax import lax
from jax.sharding import PartitionSpec as P

SEQ_LEN = 64


def grads_of(gate, up, grad_hidden):
    sig = jax.nn.sigmoid(gate)
    hidden = gate * sig * up
    grad_up = grad_hidden * gate * sig
    grad_gate = grad_hidden * up * sig * (1.0 + gate * (1.0 - sig))
    return (
        hidden.astype(jnp.bfloat16),
        grad_gate.astype(jnp.bfloat16),
        grad_up.astype(jnp.bfloat16),
    )


def outer_sums(left, right):
    count = left.shape[0] // SEQ_LEN
    left_seq = left.reshape(count, SEQ_LEN, left.shape[1])
    right_seq = right.reshape(count, SEQ_LEN, right.shape[1])
    total = jnp.einsum("stq,str->sqr", left_seq, right_seq, precision=lax.Precision.HIGHEST)
    return total.reshape(count, left.shape[1] * right.shape[1])


def query_of(in_proj, gate_proj, up_proj, hidden_proj, out_proj):
    return jnp.concatenate(
        [
            outer_sums(in_proj, gate_proj),
            outer_sums(in_proj, up_proj),
            outer_sums(hidden_proj, out_proj),
        ],
        axis=1,
    )


def local(
    acts,
    out_grad,
    w_gate,
    w_up,
    w_down,
    proj_in,
    proj_gate,
    proj_up,
    proj_hidden,
    proj_out,
    store,
    doc_ids,
):
    width = w_gate.shape[1]
    rank = proj_in.shape[1]
    contract_last = (((1,), (1,)), ((), ()))
    left_weights = jnp.concatenate([w_gate, w_up, proj_in], axis=1)
    forward = jnp.dot(acts, left_weights, preferred_element_type=jnp.float32)
    backward = lax.dot_general(out_grad, w_down, contract_last, preferred_element_type=jnp.float32)
    outward = jnp.dot(out_grad, proj_out, preferred_element_type=jnp.float32)
    summed = lax.psum_scatter(
        jnp.concatenate([forward, backward, outward], axis=1).astype(jnp.bfloat16),
        "example",
        scatter_dimension=0,
        tiled=True,
    ).astype(jnp.float32)
    gate = summed[:, :width]
    up = summed[:, width : 2 * width]
    in_proj = summed[:, 2 * width : 2 * width + rank]
    grad_hidden = summed[:, 2 * width + rank : 3 * width + rank]
    out_proj = summed[:, 3 * width + rank :]
    hidden, grad_gate, grad_up = grads_of(gate, up, grad_hidden)
    gate_part = jnp.dot(grad_gate, proj_gate, preferred_element_type=jnp.float32)
    up_part = jnp.dot(grad_up, proj_up, preferred_element_type=jnp.float32)
    hidden_part = jnp.dot(hidden, proj_hidden, preferred_element_type=jnp.float32)
    gate_proj, up_proj, hidden_proj = (
        lax.psum(gate_part.astype(jnp.bfloat16), "tensor").astype(jnp.float32),
        lax.psum(up_part.astype(jnp.bfloat16), "tensor").astype(jnp.float32),
        lax.psum(hidden_part.astype(jnp.bfloat16), "tensor").astype(jnp.float32),
    )
    own_query = query_of(in_proj, gate_proj, up_proj, hidden_proj, out_proj).astype(jnp.bfloat16)
    query = lax.all_gather(own_query, "example", axis=0, tiled=True)
    picked = jnp.take(store, doc_ids[0], axis=0)
    return lax.dot_general(query, picked, contract_last, preferred_element_type=jnp.float32)


def solution(mesh):
    return jax.shard_map(
        local,
        mesh=mesh,
        in_specs=(
            P(None, "example"),
            P(None, "example"),
            P("example", "tensor"),
            P("example", "tensor"),
            P("tensor", "example"),
            P("example", None),
            P("tensor", None),
            P("tensor", None),
            P("tensor", None),
            P("example", None),
            P(("tensor", "example"), None),
            P(("tensor", "example"), None),
        ),
        out_specs=P(None, ("tensor", "example")),
        check_vma=False,
    )
```

profile of v0, /device:TPU:0, one launch (start us, length us, event | category | flops | bytes accessed | tf_op | source)
XLA Modules:
  0.0 193.3 jit_solution(8513815710191261834)
XLA Ops:
  6.5 0.0 copy-start
  6.5 0.0 reduce-scatter.4.cloned.1.call-start
  6.5 2.1 %copy.17 = bf16[2048,64]{1,0:T(8,128)(2,1)} copy(bf16[2048,64]{0,1:T(8,128)(2,1)} %param.17) | data formatting | bytes 524288 | tf_op args[5]
  8.6 0.0 copy-start.1
  8.6 0.0 copy-start.3
  8.6 0.0 copy-start.2
  8.6 0.0 copy-start.4
  8.7 9.7 %convolution_convert_fusion = bf16[256,3584]{0,1:T(8,128)(2,1)S(1)} fusion(bf16[256,2048]{1,0:T(8,128)(2,1)} %param.13, bf16[3584,2048]{1,0:T(8,128)(2,1)} %param.16), kind=kOutput, calls=%fused_computation.10 | convolution fusion | flops 3759013888 | bytes 17563648 | tf_op jit(solution)/shard_map/dot_general | solution.py:59
  18.3 0.0 copy-done.1
  18.3 0.0 copy-done.3
  18.3 0.4 convolution_convert_fusion.1
  18.8 0.0 copy-done.2
  18.8 0.0 copy-done.4
  18.8 14.2 %fusion.9 = bf16[256,7232]{0,1:T(8,128)(2,1)S(1)} fusion(bf16[256,2048]{1,0:T(8,128)(2,1)S(1)} %copy-done.4, bf16[2048,64]{1,0:T(8,128)(2,1)S(1)} %copy-done.2, bf16[2048,3584]{1,0:T(8,128)(2,1)} %param.15, bf16[2048,3584]{1,0:T(8,128)(2,1)} %param.14), kind=kOutput, calls=%fused_computation.8 | convolution fusion | flops 7674019840 | bytes 34373632 | tf_op jit(solution)/shard_map/dot_general | solution.py:58
  33.0 25.2 %pad_maximum_fusion = bf16[256,10880]{0,1:T(8,128)(2,1)} fusion(bf16[256,64]{0,1:T(8,128)(2,1)S(1)} %convolution_convert_fusion.1, bf16[256,3584]{0,1:T(8,128)(2,1)S(1)} %convolution_convert_fusion, bf16[256,7232]{0,1:T(8,128)(2,1)S(1)} %fusion.9), kind=kLoop, calls=%fused_computation.9 | loop fusion | flops 16711680 | bytes 11141120 | tf_op jit(solution)/shard_map/concatenate | solution.py:62
  58.2 8.3 %copy.20 = bf16[256,10880]{1,0:T(8,128)(2,1)} copy(bf16[256,10880]{0,1:T(8,128)(2,1)} %pad_maximum_fusion) | data formatting | bytes 11141120
  66.5 0.0 copy-start.8
  66.5 0.0 reduce-scatter.4.cloned.1.call-update
  66.5 0.6 copy-done.8
  67.2 0.0 copy-done
  67.2 4.2 %gather_fusion = bf16[128,12288]{1,0:T(8,128)(2,1)} fusion(bf16[128,12288]{1,0:T(8,128)(2,1)S(1)} %copy-done, s32[1024]{0:T(1024)S(1)} %pad_clamp_fusion), kind=kCustom, calls=%fused_computation | custom fusion | bytes 6291968 | tf_op jit(solution)/shard_map/jit(_take)/gather | solution.py:83
  71.4 62.1 %reduce-scatter.4.cloned.1.call-done = bf16[64,10880]{1,0:T(8,128)(2,1)} async-done(((bf16[256,10880]{1,0:T(8,128)(2,1)}), bf16[64,10880]{1,0:T(8,128)(2,1)}) %reduce-scatter.4.cloned.1.call-update) | async-done | bytes 1392656
  133.5 4.0 %copy.21 = bf16[64,10880]{0,1:T(8,128)(2,1)} copy(bf16[64,10880]{1,0:T(8,128)(2,1)} %reduce-scatter.4.cloned.1.call-done) | data formatting | bytes 2785280
  137.5 0.0 copy-start.5
  137.5 2.0 %convert_element_type.34 = f32[64,10880]{0,1:T(8,128)S(1)} convert(bf16[64,10880]{0,1:T(8,128)(2,1)} %copy.21) | non-fusion elementwise | flops 696320 | bytes 4177920 | tf_op jit(solution)/shard_map/convert_element_type | solution.py:66
  139.5 0.0 copy-done.5
  139.6 0.0 copy-start.6
  139.6 0.7 convolution_convert_fusion.2
  140.3 0.3 copy-done.6
  140.6 0.0 copy-start.7
  140.6 0.7 convolution_convert_fusion.3
  141.3 0.3 copy-done.7
  141.6 0.9 convolution_convert_fusion.4
  142.5 29.0 %all-reduce = (bf16[64,64]{1,0:T(8,128)(2,1)S(1)}, bf16[64,64]{1,0:T(8,128)(2,1)S(1)}, bf16[64,64]{1,0:T(8,128)(2,1)S(1)}) all-reduce(bf16[64,64]{1,0:T(8,128)(2,1)S(1)} %convolution_convert_fusion.2, bf16[64,64]{1,0:T(8,128)(2,1)S(1)} %convolution_convert_fusion.3, ...), channel_id=1, replica_groups=mesh['tensor'=8,'example'=4] {'tensor'}, use_global_device_ids=true, to_apply=%region_3.0 | all-reduce | flops 12288 | bytes 49152 | tf_op jit(solution)/shard_map/psum | solution.py:79
  171.5 0.8 convolution_convert_fusion.7
  172.4 0.1 concatenate.27
  172.5 0.8 convolution_convert_fusion.6
  173.3 0.1 concatenate.28
  173.4 0.9 convolution_convert_fusion.5
  174.3 0.1 concatenate.29
  174.4 0.1 maximum_bitcast_fusion
  174.5 8.5 %all-gather = bf16[4,1,12288]{2,1,0:T(2,128)(2,1)S(1)} all-gather(bf16[1,1,12288]{2,1,0:T(2,128)(2,1)S(1)} %maximum_bitcast_fusion), channel_id=1, replica_groups=mesh['tensor'=8,'example'=4] {'example'}, dimensions={0}, use_global_device_ids=true | all-gather | bytes 122880 | tf_op jit(solution)/shard_map/all_gather | solution.py:82
  183.0 3.5 %fusion.12 = f32[4,128]{1,0:T(4,128)} fusion(bf16[128,12288]{1,0:T(8,128)(2,1)} %gather_fusion, pred[128]{0:T(512)(128)(4,1)S(1)} %compare_and_fusion, bf16[4,1,12288]{2,1,0:T(2,128)(2,1)S(1)} %all-gather), kind=kOutput, calls=%fused_computation.11 | convolution fusion | flops 14155776 | bytes 3246208 | tf_op jit(solution)/shard_map/dot_general | solution.py:84
  (3 shorter events, 0.0 us)
Async XLA Ops:
  6.5 60.6 %copy-start = (bf16[128,12288]{1,0:T(8,128)(2,1)S(1)}, bf16[128,12288]{1,0:T(8,128)(2,1)}, u32[]{:S(2)}) copy-start(bf16[128,12288]{1,0:T(8,128)(2,1)} %param.22) | copy-start | bytes 9437188
  6.5 127.0 %reduce-scatter.4.cloned.1.call-start = ((), (), s32[]{:S(2)}) async-start(), calls=%async_computation.1 | async-start | bytes 6963200
  8.6 9.7 %copy-start.1 = (bf16[256,2048]{1,0:T(8,128)(2,1)S(1)}, bf16[256,2048]{1,0:T(8,128)(2,1)}, u32[]{:S(2)}) copy-start(bf16[256,2048]{1,0:T(8,128)(2,1)} %param.13) | copy-start | bytes 3145732
  8.6 9.7 %copy-start.3 = (bf16[2048,64]{0,1:T(8,128)(2,1)S(1)}, bf16[2048,64]{0,1:T(8,128)(2,1)}, u32[]{:S(2)}) copy-start(bf16[2048,64]{0,1:T(8,128)(2,1)} %param.21) | copy-start | bytes 786436
  8.6 10.1 %copy-start.2 = (bf16[2048,64]{1,0:T(8,128)(2,1)S(1)}, bf16[2048,64]{1,0:T(8,128)(2,1)}, u32[]{:S(2)}) copy-start(bf16[2048,64]{1,0:T(8,128)(2,1)} %copy.17) | copy-start | bytes 786436
  8.6 10.2 %copy-start.4 = (bf16[256,2048]{1,0:T(8,128)(2,1)S(1)}, bf16[256,2048]{1,0:T(8,128)(2,1)}, u32[]{:S(2)}) copy-start(bf16[256,2048]{1,0:T(8,128)(2,1)} %param.12) | copy-start | bytes 3145732
  66.5 0.7 copy-start.8
  137.5 2.0 %copy-start.5 = (bf16[3584,64]{0,1:T(8,128)(2,1)S(1)}, bf16[3584,64]{0,1:T(8,128)(2,1)}, u32[]{:S(2)}) copy-start(bf16[3584,64]{0,1:T(8,128)(2,1)} %param.20) | copy-start | bytes 1376260
  139.6 1.0 copy-start.6
  140.6 1.0 copy-start.7
Sparse Core Ops, SparseCore 0:
  66.6 66.8 reduce-scatter.3
where the time goes:
time: 194 us; the launch traced here: 193 us
  waiting for transfers between devices  62.2 us (32%)
  blocking collectives  37.6 us (19%)
  matrix products  32.7 us (17%)
  other arithmetic  27.3 us (14%)
  local copies, waits for them, and re-layouts  20.1 us (10%)
  between operations  13.5 us (7%)
    unnamed x2, waiting for transfers between devices  62.2 us
    psum x1, blocking collectives, local(): lax.psum(hidden_part.astype(jnp.bfloat16), 'tensor').astype(jnp.float32)  29 us
    concatenate x1, other arithmetic, local(): jnp.concatenate([forward, backward, outward], axis=1).astype(jnp.bfloat16)  25.2 us
    unnamed x21, local copies, waits for them, and re-layouts  15.6 us
    dot_general x1, matrix products, local(): forward = jnp.dot(acts, left_weights, preferred_element_type=jnp.float32)  14.2 us
    dot_general x1, matrix products, local(): lax.dot_general(out_grad, w_down, contract_last, preferred_element_type=j...  9.66 us
    all_gather x1, blocking collectives, local(): query = lax.all_gather(own_query, 'example', axis=0, tiled=True)  8.53 us
    gather x1, local copies, waits for them, and re-layouts, local(): picked = jnp.take(store, doc_ids[0], axis=0)  4.22 us
  transfers between devices with their start and end apart: 1, of which 1 were waited for; matrix products, arithmetic and copies ran while one was open for 2% of the time, Pallas kernels for 0%

commit v1 on v0

v1 whole, which is shorter than its diff:
```python
import functools

import jax
import jax.numpy as jnp
from jax import lax
from jax.experimental import pallas as pl
from jax.experimental.pallas import tpu as pltpu
from jax.sharding import PartitionSpec as P

SEQ_LEN = 64
NT = (((1,), (1,)), ((), ()))
TN = (((0,), (0,)), ((), ()))
F32 = jnp.float32
BF16 = jnp.bfloat16


def chunk_steps(total):
    if total == 14:
        return [1, 2, 3, 3, 3, 2]
    chunks, left = [1], total - 1
    while left:
        chunks.append(min(2, left))
        left -= chunks[-1]
    return chunks


def partials_kernel(count, bit, extra, width, e_ref, *refs):
    acts = jnp.concatenate([refs[j][...] for j in range(count)], axis=0)
    grads = jnp.concatenate([refs[count + j][...] for j in range(count)], axis=0)
    refs = refs[2 * count :]
    w_gate, w_up, w_down = refs[:3]
    send, keep = refs[-2:]
    parts = [
        jnp.dot(acts, w_gate[...], preferred_element_type=F32),
        jnp.dot(acts, w_up[...], preferred_element_type=F32),
        lax.dot_general(grads, w_down[...], NT, preferred_element_type=F32),
    ]
    if extra:
        parts.append(
            jnp.concatenate(
                [
                    lax.dot_general(acts, refs[3][...], NT, preferred_element_type=F32),
                    lax.dot_general(grads, refs[4][...], NT, preferred_element_type=F32),
                ],
                axis=1,
            )
        )
    at = 0
    for part in parts:
        value = part.astype(BF16)
        place = [0, 0]
        for j in range(count):
            goes = 1 if j & bit else 0
            out = send if goes else keep
            rows = pl.ds(place[goes] * SEQ_LEN, SEQ_LEN)
            out[0, rows, at : at + value.shape[1]] = value[j * SEQ_LEN : (j + 1) * SEQ_LEN]
            place[goes] += 1
        at += value.shape[1]


def partials(index, acts, grads, w_gate, w_up, w_down, extras, first, steps, width, bit):
    depth = acts.shape[1]
    count = acts.shape[0] // SEQ_LEN
    extra = len(extras) > 0
    columns = 3 * width + (2 * extras[0].shape[0] if extra else 0)
    rows = [
        pl.BlockSpec((SEQ_LEN, depth), functools.partial(lambda j, i, e: (e[0] ^ j, 0), j))
        for j in range(count)
    ]
    half = (1, count // 2 * SEQ_LEN, columns)
    shape = jax.ShapeDtypeStruct((steps,) + half[1:], BF16)
    return pl.pallas_call(
        functools.partial(partials_kernel, count, bit, extra, width),
        out_shape=(shape, shape),
        grid_spec=pltpu.PrefetchScalarGridSpec(
            num_scalar_prefetch=1,
            grid=(steps,),
            in_specs=rows
            + rows
            + [
                pl.BlockSpec((depth, width), lambda i, e: (0, first + i)),
                pl.BlockSpec((depth, width), lambda i, e: (0, first + i)),
                pl.BlockSpec((width, depth), lambda i, e: (first + i, 0)),
            ]
            + [pl.BlockSpec(x.shape, lambda i, e: (0, 0)) for x in extras],
            out_specs=[pl.BlockSpec(half, lambda i, e: (i, 0, 0))] * 2,
        ),
        compiler_params=pltpu.CompilerParams(vmem_limit_bytes=32 << 20),
        name=f"partials_{first}",
    )(index, *([acts] * count), *([grads] * count), w_gate, w_up, w_down, *extras)


def project_kernel(terms, width, *refs):
    addends, (p_gate, p_up, p_hidden, before, after) = refs[:terms], refs[terms:]
    total = functools.reduce(
        jnp.add, [ref[0, :, : 3 * width].astype(F32) for ref in addends]
    )
    gate = total[:, :width]
    up = total[:, width : 2 * width]
    back = total[:, 2 * width :]
    sig = jax.nn.sigmoid(gate)
    gs = gate * sig
    hidden = (gs * up).astype(BF16)
    grad_up = (back * gs).astype(BF16)
    grad_gate = (back * up * sig * (1.0 + gate * (1.0 - sig))).astype(BF16)
    part = jnp.concatenate(
        [
            lax.dot_general(grad_gate, p_gate[...], NT, preferred_element_type=F32),
            lax.dot_general(grad_up, p_up[...], NT, preferred_element_type=F32),
            lax.dot_general(hidden, p_hidden[...], NT, preferred_element_type=F32),
        ],
        axis=1,
    )

    @pl.when(pl.program_id(0) == 0)
    def _():
        after[...] = before[...] + part

    @pl.when(pl.program_id(0) != 0)
    def _():
        after[...] += part


def project(addends, projections, before, first, width):
    steps, _, columns = addends[0].shape
    rank = projections[0].shape[0]
    return pl.pallas_call(
        functools.partial(project_kernel, len(addends), width),
        out_shape=jax.ShapeDtypeStruct(before.shape, F32),
        grid=(steps,),
        in_specs=[pl.BlockSpec((1, SEQ_LEN, columns), lambda i: (i, 0, 0))] * len(addends)
        + [pl.BlockSpec((rank, width), lambda i: (0, first + i))] * 3
        + [pl.BlockSpec(before.shape, lambda i: (0, 0))],
        out_specs=pl.BlockSpec(before.shape, lambda i: (0, 0)),
        compiler_params=pltpu.CompilerParams(vmem_limit_bytes=16 << 20),
        name=f"project_{first}",
    )(*addends, *projections, before)


def outer_kernel(terms, at, rank, *refs):
    sums, projected, out = refs[:terms], refs[terms], refs[terms + 1]
    both = functools.reduce(jnp.add, [r[0, :, at : at + 2 * rank].astype(F32) for r in sums])
    in_proj, out_proj = both[:, :rank], both[:, rank:]
    gate_up = projected[:, : 2 * rank]
    hidden = projected[:, 2 * rank :]

    def dot(a, b):
        return lax.dot_general(
            a, b, TN, preferred_element_type=F32, precision=lax.Precision.HIGHEST
        )

    out[:, : 2 * rank] = dot(in_proj, gate_up).astype(BF16)
    out[:, 2 * rank :] = dot(hidden, out_proj).astype(BF16)


def outer(sums, projected, at, rank):
    columns = sums[0].shape[2]
    return pl.pallas_call(
        functools.partial(outer_kernel, len(sums), at, rank),
        out_shape=jax.ShapeDtypeStruct((rank, 3 * rank), BF16),
        grid=(1,),
        in_specs=[pl.BlockSpec((1, SEQ_LEN, columns), lambda i: (0, 0, 0))] * len(sums)
        + [pl.BlockSpec(projected.shape, lambda i: (0, 0))],
        out_specs=pl.BlockSpec((rank, 3 * rank), lambda i: (0, 0)),
        compiler_params=pltpu.CompilerParams(vmem_limit_bytes=16 << 20),
        name="outer",
    )(*sums, projected)


def score_kernel(count, e_ref, *refs):
    queries, (store, ids, out, rows) = refs[:count], refs[count:]
    for j in range(count):
        rows[pl.ds(e_ref[0] ^ j, 1), :] = queries[j][...].astype(F32)
    lhs = rows[...].astype(BF16)
    natural = lax.dot_general(lhs, store[...], NT, preferred_element_type=F32)
    docs = store.shape[0]
    chosen = lax.broadcasted_iota(jnp.int32, (docs, docs), 0) == ids[...]
    out[...] = jnp.dot(
        natural, chosen.astype(F32), preferred_element_type=F32, precision=lax.Precision.HIGHEST
    )


def score(index, queries, store, ids):
    count = len(queries)
    docs, size = store.shape
    vmem = pl.BlockSpec(memory_space=pltpu.VMEM)
    return pl.pallas_call(
        functools.partial(score_kernel, count),
        out_shape=jax.ShapeDtypeStruct((count, docs), F32),
        in_specs=[pl.BlockSpec(memory_space=pltpu.SMEM)] + [vmem] * (count + 2),
        out_specs=vmem,
        scratch_shapes=[pltpu.VMEM((count, size), F32)],
        compiler_params=pltpu.CompilerParams(vmem_limit_bytes=16 << 20),
        name="score",
    )(index, *queries, store, ids)


def local(
    sizes,
    acts,
    out_grad,
    w_gate,
    w_up,
    w_down,
    proj_in,
    proj_gate,
    proj_up,
    proj_hidden,
    proj_out,
    store,
    doc_ids,
):
    tensor, example = sizes
    units = w_gate.shape[1]
    rank = proj_in.shape[1]
    width = 256 if units % 256 == 0 else 128
    index = lax.axis_index("example").astype(jnp.int32).reshape(1)

    def flip(x, axis, k):
        n = tensor if axis == "tensor" else example
        return lax.ppermute(x, axis, [(i, i ^ k) for i in range(n)])

    bits = [1 << b for b in range(example.bit_length() - 1)]
    extras = (proj_in.T, proj_out.T)
    projections = (proj_gate.T, proj_up.T, proj_hidden.T)

    chunks = chunk_steps(units // width)
    ready = []
    first = 0
    for number, steps in enumerate(chunks):
        order = bits if number % 2 == 0 else bits[::-1]
        extra = extras if number == 0 else ()
        send, keep = partials(
            index, acts, out_grad, w_gate, w_up, w_down, extra, first, steps, width, order[0]
        )
        blocks = [j for j in range(example) if not j & order[0]]
        addends = [keep, flip(send, "example", order[0])]
        for bit in order[1:]:
            blocks_of = lambda x, keepers: jnp.concatenate(
                [
                    x[:, i * SEQ_LEN : (i + 1) * SEQ_LEN]
                    for i, j in enumerate(blocks)
                    if bool(j & bit) != keepers
                ],
                axis=1,
            )
            summed = lambda keepers: functools.reduce(
                jnp.add, [blocks_of(x, keepers).astype(F32) for x in addends]
            ).astype(BF16)
            send = summed(False)
            blocks = [j for j in blocks if not j & bit]
            if len(blocks) > 1:
                addends = [summed(True)]
            addends.append(flip(send, "example", bit))
        ready.append((addends, first))
        first += steps

    total = jnp.zeros((SEQ_LEN, 3 * rank), F32)
    for addends, first in ready:
        total = project(addends, projections, total, first, width)
    part = outer(ready[0][0], total, 3 * width, rank)

    pair = (part.astype(F32) + flip(part, "tensor", 1).astype(F32)).astype(BF16)
    whole = functools.reduce(
        jnp.add, [pair.astype(F32)] + [flip(pair, "tensor", k).astype(F32) for k in range(2, tensor, 2)]
    ).astype(BF16)
    query = jnp.concatenate(
        [whole[:, m * rank : (m + 1) * rank].reshape(1, rank * rank) for m in range(3)], axis=1
    )
    queries = [query] + [flip(query, "example", k) for k in range(1, example)]
    return score(index, queries, store, doc_ids)


def solution(mesh):
    return jax.shard_map(
        functools.partial(local, (mesh.shape["tensor"], mesh.shape["example"])),
        mesh=mesh,
        in_specs=(
            P(None, "example"),
            P(None, "example"),
            P("example", "tensor"),
            P("example", "tensor"),
            P("tensor", "example"),
            P("example", None),
            P("tensor", None),
            P("tensor", None),
            P("tensor", None),
            P("example", None),
            P(("tensor", "example"), None),
            P(("tensor", "example"), None),
        ),
        out_specs=P(None, ("tensor", "example")),
        check_vma=False,
    )
```

time: 194 us -> 92.7 us (0.48)
  blocking collectives: 37.6 us -> 0 us
  waiting for transfers between devices: 62.2 us -> 27.9 us
  matrix products: 32.7 us -> 0 us
  Pallas kernels: 0 us -> 32.3 us
  other arithmetic: 27.3 us -> 0.37 us
  starting transfers between devices: 0.01 us -> 21.5 us
  between operations: 13.5 us -> 0.27 us
  local copies, waits for them, and re-layouts: 20.1 us -> 9.97 us
    unnamed x2 -> x0, waiting for transfers between devices: 62.2 us -> none
    dot_general x10 -> x0, matrix products: 32.7 us -> none  [the longest x1 14.2 us: local(): forward = jnp.dot(acts, left_weights, preferred_element_type=jnp.float32)]
    pallas_call x0 -> x14, Pallas kernels: none -> 32.3 us  [the longest x6 26.7 us: partials(): pl.pallas_call(functools.partial(partials_kernel, count, bit, extra, widt...]
    psum x1 -> x0, blocking collectives: 29 us -> none  [local(): lax.psum(hidden_part.astype(jnp.bfloat16), 'tensor').astype(jnp.float32)]
    ppermute x0 -> x19, waiting for transfers between devices: none -> 27.9 us  [flip(): return lax.ppermute(x, axis, [(i, i ^ k) for i in range(n)])]
    concatenate x1 -> x0, other arithmetic: 25.2 us -> none  [local(): jnp.concatenate([forward, backward, outward], axis=1).astype(jnp.bfloat16)]
    ppermute x0 -> x19, starting transfers between devices: none -> 21.5 us  [flip(): return lax.ppermute(x, axis, [(i, i ^ k) for i in range(n)])]
    all_gather x1 -> x0, blocking collectives: 8.53 us -> none  [local(): query = lax.all_gather(own_query, 'example', axis=0, tiled=True)]
  transfers between devices with their start and end apart: 1 -> 19, of which waited for: 1 -> 12; matrix products, arithmetic and copies ran while one was open for 2% -> 0% of each run, Pallas kernels for 0% -> 29%
where the time goes in v1:
time: 92.7 us; the launch traced here: 92.3 us
  Pallas kernels  32.3 us (35%)
  waiting for transfers between devices  27.9 us (30%)
  starting transfers between devices  21.5 us (23%)
  local copies, waits for them, and re-layouts  9.97 us (11%)
    ppermute x19, waiting for transfers between devices, flip(): return lax.ppermute(x, axis, [(i, i ^ k) for i in range(n)])  27.9 us
    pallas_call x6, Pallas kernels, partials(): pl.pallas_call(functools.partial(partials_kernel, count, bit, extra, widt...  26.7 us
    ppermute x19, starting transfers between devices, flip(): return lax.ppermute(x, axis, [(i, i ^ k) for i in range(n)])  21.5 us
    unnamed x22, local copies, waits for them, and re-layouts  9.6 us
    pallas_call x6, Pallas kernels, project(): pl.pallas_call(functools.partial(project_kernel, len(addends), width), ou...  3.61 us
  transfers between devices with their start and end apart: 19, of which 12 were waited for; matrix products, arithmetic and copies ran while one was open for 0% of the time, Pallas kernels for 29%

profile of v1, /device:TPU:0, one launch (start us, length us, event | category | flops | bytes accessed | tf_op | source)
XLA Modules:
  0.0 92.3 jit_solution(2803511314364607573)
XLA Ops:
  0.0 1.2 %copy-done = bf16[256,2048]{1,0:T(8,128)(2,1)S(1)} copy-done((bf16[256,2048]{1,0:T(8,128)(2,1)S(1)}, bf16[256,2048]{1,0:T(8,128)(2,1)}, u32[]{:S(2)}) %copy-start) | copy-done | bytes 1048600
  1.2 1.2 %copy-done.1 = bf16[256,2048]{1,0:T(8,128)(2,1)S(1)} copy-done((bf16[256,2048]{1,0:T(8,128)(2,1)S(1)}, bf16[256,2048]{1,0:T(8,128)(2,1)}, u32[]{:S(2)}) %copy-start.1) | copy-done | bytes 1048600
  2.5 5.2 %copy-done.2 = bf16[2048,3584]{1,0:T(8,128)(2,1)S(1)} copy-done((bf16[2048,3584]{1,0:T(8,128)(2,1)S(1)}, bf16[2048,3584]{1,0:T(8,128)(2,1)}, u32[]{:S(2)}) %copy-start.2) | copy-done | bytes 14680088
  7.6 0.9 %copy-done.7 = bf16[2048,64]{0,1:T(8,128)(2,1)S(1)} copy-done((bf16[2048,64]{0,1:T(8,128)(2,1)S(1)}, bf16[2048,64]{0,1:T(8,128)(2,1)}, u32[]{:S(2)}) %copy-start.7) | copy-done | bytes 262168
  8.6 0.9 %copy-done.8 = bf16[2048,64]{0,1:T(8,128)(2,1)S(1)} copy-done((bf16[2048,64]{0,1:T(8,128)(2,1)S(1)}, bf16[2048,64]{0,1:T(8,128)(2,1)}, u32[]{:S(2)}) %copy-start.8) | copy-done | bytes 262168
  9.5 3.3 %partials_0.1 = (bf16[1,128,896]{2,1,0:T(8,128)(2,1)S(1)}, bf16[1,128,896]{2,1,0:T(8,128)(2,1)S(1)}) custom-call(s32[1]{0:T(128)} %bitcast.e_ref, bf16[256,2048]{1,0:T(8,128)(2,1)S(1)} %copy-done, bf16[256,2048]{1,0:T(8,128)(2,1)S(1)} %copy-done, bf16[256,2048]{1,0:T(8,128)(2,1)S(1)} %copy-done, bf16[256,2048]{1,0:T(8,128)(2,1)S(1)} %copy-done, ...), custom_call_target="tpu_custom_call" | custom-call | tf_op jit(solution)/shard_map/partials_0/pallas_call | solution.py:72
  12.8 3.0 %collective-permute-start = (bf16[1,128,896]{2,1,0:T(8,128)(2,1)S(1)}, bf16[1,128,896]{2,1,0:T(8,128)(2,1)S(1)}, u32[]{:S(2)}, u32[]{:S(2)}) collective-permute-start(bf16[1,128,896]{2,1,0:T(8,128)(2,1)S(1)} %get-tuple-element.18), channel_id=1, source_target_pairs={{0,1},{1,0},{2,3},{3,2},{4,5},{5,4},{6,7},{7,6},{8,9},{9,8},{10,11... | collective-permute-start | bytes 688136 | tf_op jit(solution)/shard_map/ppermute | solution.py:221
  15.8 3.7 %partials_1.1 = (bf16[2,128,768]{2,1,0:T(8,128)(2,1)S(1)}, bf16[2,128,768]{2,1,0:T(8,128)(2,1)S(1)}) custom-call(s32[1]{0:T(128)} %bitcast.e_ref, bf16[256,2048]{1,0:T(8,128)(2,1)S(1)} %copy-done, bf16[256,2048]{1,0:T(8,128)(2,1)S(1)} %copy-done, bf16[256,2048]{1,0:T(8,128)(2,1)S(1)} %copy-done, bf16[256,2048]{1,0:T(8,128)(2,1)S(1)} %copy-done, ...), custom_call_target="tpu_custom_call" | custom-call | tf_op jit(solution)/shard_map/partials_1/pallas_call | solution.py:72
  19.5 1.6 %collective-permute-start.10 = (bf16[2,128,768]{2,1,0:T(8,128)(2,1)S(1)}, bf16[2,128,768]{2,1,0:T(8,128)(2,1)S(1)}, u32[]{:S(2)}, u32[]{:S(2)}) collective-permute-start(bf16[2,128,768]{2,1,0:T(8,128)(2,1)S(1)} %get-tuple-element.28), channel_id=1, source_target_pairs={{0,2},{1,3},{2,0},{3,1},{4,6},{5,7},{6,4},{7,5},{8,10},{9,11},{10,... | collective-permute-start | bytes 1179656 | tf_op jit(solution)/shard_map/ppermute | solution.py:221
  21.1 5.3 %partials_3.1 = (bf16[3,128,768]{2,1,0:T(8,128)(2,1)S(1)}, bf16[3,128,768]{2,1,0:T(8,128)(2,1)S(1)}) custom-call(s32[1]{0:T(128)} %bitcast.e_ref, bf16[256,2048]{1,0:T(8,128)(2,1)S(1)} %copy-done, bf16[256,2048]{1,0:T(8,128)(2,1)S(1)} %copy-done, bf16[256,2048]{1,0:T(8,128)(2,1)S(1)} %copy-done, bf16[256,2048]{1,0:T(8,128)(2,1)S(1)} %copy-done, ...), custom_call_target="tpu_custom_call" | custom-call | tf_op jit(solution)/shard_map/partials_3/pallas_call | solution.py:72
  26.4 0.6 collective-permute-start.8
  27.1 5.3 %partials_6.1 = (bf16[3,128,768]{2,1,0:T(8,128)(2,1)S(1)}, bf16[3,128,768]{2,1,0:T(8,128)(2,1)S(1)}) custom-call(s32[1]{0:T(128)} %bitcast.e_ref, bf16[256,2048]{1,0:T(8,128)(2,1)S(1)} %copy-done, bf16[256,2048]{1,0:T(8,128)(2,1)S(1)} %copy-done, bf16[256,2048]{1,0:T(8,128)(2,1)S(1)} %copy-done, bf16[256,2048]{1,0:T(8,128)(2,1)S(1)} %copy-done, ...), custom_call_target="tpu_custom_call" | custom-call | tf_op jit(solution)/shard_map/partials_6/pallas_call | solution.py:72
  32.4 0.1 collective-permute-start.6
  32.5 5.3 %partials_9.1 = (bf16[3,128,768]{2,1,0:T(8,128)(2,1)S(1)}, bf16[3,128,768]{2,1,0:T(8,128)(2,1)S(1)}) custom-call(s32[1]{0:T(128)} %bitcast.e_ref, bf16[256,2048]{1,0:T(8,128)(2,1)S(1)} %copy-done, bf16[256,2048]{1,0:T(8,128)(2,1)S(1)} %copy-done, bf16[256,2048]{1,0:T(8,128)(2,1)S(1)} %copy-done, bf16[256,2048]{1,0:T(8,128)(2,1)S(1)} %copy-done, ...), custom_call_target="tpu_custom_call" | custom-call | tf_op jit(solution)/shard_map/partials_9/pallas_call | solution.py:72
  37.9 2.0 %collective-permute-start.4 = (bf16[3,128,768]{2,1,0:T(8,128)(2,1)S(1)}, bf16[3,128,768]{2,1,0:T(8,128)(2,1)S(1)}, u32[]{:S(2)}, u32[]{:S(2)}) collective-permute-start(bf16[3,128,768]{2,1,0:T(8,128)(2,1)S(1)} %get-tuple-element.22), channel_id=1, source_target_pairs={{0,1},{1,0},{2,3},{3,2},{4,5},{5,4},{6,7},{7,6},{8,9},{9,8},{10,11... | collective-permute-start | bytes 1769480 | tf_op jit(solution)/shard_map/ppermute | solution.py:221
  39.9 3.7 %partials_12.1 = (bf16[2,128,768]{2,1,0:T(8,128)(2,1)S(1)}, bf16[2,128,768]{2,1,0:T(8,128)(2,1)S(1)}) custom-call(s32[1]{0:T(128)} %bitcast.e_ref, bf16[256,2048]{1,0:T(8,128)(2,1)S(1)} %copy-done, bf16[256,2048]{1,0:T(8,128)(2,1)S(1)} %copy-done, bf16[256,2048]{1,0:T(8,128)(2,1)S(1)} %copy-done, bf16[256,2048]{1,0:T(8,128)(2,1)S(1)} %copy-done, ...), custom_call_target="tpu_custom_call" | custom-call | tf_op jit(solution)/shard_map/partials_12/pallas_call | solution.py:72
  43.7 1.6 %collective-permute-start.2 = (bf16[2,128,768]{2,1,0:T(8,128)(2,1)S(1)}, bf16[2,128,768]{2,1,0:T(8,128)(2,1)S(1)}, u32[]{:S(2)}, u32[]{:S(2)}) collective-permute-start(bf16[2,128,768]{2,1,0:T(8,128)(2,1)S(1)} %get-tuple-element.20), channel_id=1, source_target_pairs={{0,2},{1,3},{2,0},{3,1},{4,6},{5,7},{6,4},{7,5},{8,10},{9,11},{10,... | collective-permute-start | bytes 1179656 | tf_op jit(solution)/shard_map/ppermute | solution.py:221
  45.3 0.6 collective-permute-start.1
  45.9 0.3 collective-permute-start.11
  46.3 2.2 %collective-permute-done.6.refs_1_ = bf16[3,128,768]{2,1,0:T(8,128)(2,1)S(1)} collective-permute-done((bf16[3,128,768]{2,1,0:T(8,128)(2,1)S(1)}, bf16[3,128,768]{2,1,0:T(8,128)(2,1)S(1)}, u32[]{:S(2)}, u32[]{:S(2)}) %collective-permute-start.6) | collective-permute-done | bytes 589856 | tf_op jit(solution)/shard_map/ppermute | solution.py:221
  48.6 6.5 %collective-permute-done.4.refs_1_ = bf16[3,128,768]{2,1,0:T(8,128)(2,1)S(1)} collective-permute-done((bf16[3,128,768]{2,1,0:T(8,128)(2,1)S(1)}, bf16[3,128,768]{2,1,0:T(8,128)(2,1)S(1)}, u32[]{:S(2)}, u32[]{:S(2)}) %collective-permute-start.4) | collective-permute-done | bytes 589856 | tf_op jit(solution)/shard_map/ppermute | solution.py:221
  55.1 1.1 %collective-permute-start.7 = (bf16[3,64,768]{2,1,0:T(8,128)(2,1)S(1)}, bf16[3,64,768]{2,1,0:T(8,128)(2,1)S(1)}, u32[]{:S(2)}, u32[]{:S(2)}) collective-permute-start(bf16[3,64,768]{2,1,0:T(8,128)(2,1)S(1)} %add_convert_fusion.1), channel_id=1, source_target_pairs={{0,1},{1,0},{2,3},{3,2},{4,5},{5,4},{6,7},{7,6},{8,9},{9,8},{10,11... | collective-permute-start | bytes 884744 | tf_op jit(solution)/shard_map/ppermute | solution.py:221
  56.2 0.7 collective-permute-done.2.refs_1_
  57.0 0.9 collective-permute-start.5
  57.9 1.5 %collective-permute-done.1.refs_2_ = bf16[1,64,896]{2,1,0:T(8,128)(2,1)S(1)} collective-permute-done((bf16[1,64,896]{2,1,0:T(8,128)(2,1)S(1)}, bf16[1,64,896]{2,1,0:T(8,128)(2,1)S(1)}, u32[]{:S(2)}, u32[]{:S(2)}) %collective-permute-start.1) | collective-permute-done | bytes 114720 | tf_op jit(solution)/shard_map/ppermute | solution.py:221
  59.4 1.7 %collective-permute-start.3 = (bf16[2,64,768]{2,1,0:T(8,128)(2,1)S(1)}, bf16[2,64,768]{2,1,0:T(8,128)(2,1)S(1)}, u32[]{:S(2)}, u32[]{:S(2)}) collective-permute-start(bf16[2,64,768]{2,1,0:T(8,128)(2,1)S(1)} %add_convert_fusion.4), channel_id=1, source_target_pairs={{0,1},{1,0},{2,3},{3,2},{4,5},{5,4},{6,7},{7,6},{8,9},{9,8},{10,11... | collective-permute-start | bytes 589832 | tf_op jit(solution)/shard_map/ppermute | solution.py:221
  61.1 0.2 project_0.1.refs_6_
  61.4 0.5 project_1.1.refs_6_
  61.9 3.8 %collective-permute-done.9.refs_2_ = bf16[3,64,768]{2,1,0:T(8,128)(2,1)S(1)} collective-permute-done((bf16[3,64,768]{2,1,0:T(8,128)(2,1)S(1)}, bf16[3,64,768]{2,1,0:T(8,128)(2,1)S(1)}, u32[]{:S(2)}, u32[]{:S(2)}) %collective-permute-start.9) | collective-permute-done | bytes 294944 | tf_op jit(solution)/shard_map/ppermute | solution.py:221
  65.7 0.8 project_3.1.refs_6_
  66.5 0.8 project_6.1.refs_6_
  67.3 2.9 %collective-permute-done.5.refs_2_ = bf16[3,64,768]{2,1,0:T(8,128)(2,1)S(1)} collective-permute-done((bf16[3,64,768]{2,1,0:T(8,128)(2,1)S(1)}, bf16[3,64,768]{2,1,0:T(8,128)(2,1)S(1)}, u32[]{:S(2)}, u32[]{:S(2)}) %collective-permute-start.5) | collective-permute-done | bytes 294944 | tf_op jit(solution)/shard_map/ppermute | solution.py:221
  70.2 0.8 project_9.1.refs_6_
  71.0 0.5 project_12.1.refs_3_
  71.5 0.3 outer.1
  71.9 1.2 %collective-permute-done.12 = bf16[64,192]{1,0:T(8,128)(2,1)S(1)} collective-permute-done((bf16[64,192]{1,0:T(8,128)(2,1)S(1)}, bf16[64,192]{1,0:T(8,128)(2,1)S(1)}, u32[]{:S(2)}, u32[]{:S(2)}) %collective-permute-start.12) | collective-permute-done | bytes 24608 | tf_op jit(solution)/shard_map/ppermute | solution.py:221
  73.1 1.6 %collective-permute-start.13 = (bf16[64,192]{1,0:T(8,128)(2,1)S(1)}, bf16[64,192]{1,0:T(8,128)(2,1)S(1)}, u32[]{:S(2)}, u32[]{:S(2)}) collective-permute-start(bf16[64,192]{1,0:T(8,128)(2,1)S(1)} %add_convert_fusion.7), channel_id=1, source_target_pairs={{0,8},{4,12},{8,0},{12,4},{16,24},{20,28},{24,16},{28,20},{1,9},{5... | collective-permute-start | bytes 73736 | tf_op jit(solution)/shard_map/ppermute | solution.py:221
  74.8 2.6 %collective-permute-start.14 = (bf16[64,192]{1,0:T(8,128)(2,1)S(1)}, bf16[64,192]{1,0:T(8,128)(2,1)S(1)}, u32[]{:S(2)}, u32[]{:S(2)}) collective-permute-start(bf16[64,192]{1,0:T(8,128)(2,1)S(1)} %add_convert_fusion.7), channel_id=1, source_target_pairs={{0,16},{4,20},{8,24},{12,28},{16,0},{20,4},{24,8},{28,12},{1,17},{... | collective-permute-start | bytes 73736 | tf_op jit(solution)/shard_map/ppermute | solution.py:221
  77.3 0.2 collective-permute-start.15
  77.6 2.6 %collective-permute-done.14 = bf16[64,192]{1,0:T(8,128)(2,1)S(1)} collective-permute-done((bf16[64,192]{1,0:T(8,128)(2,1)S(1)}, bf16[64,192]{1,0:T(8,128)(2,1)S(1)}, u32[]{:S(2)}, u32[]{:S(2)}) %collective-permute-start.14) | collective-permute-done | bytes 24608 | tf_op jit(solution)/shard_map/ppermute | solution.py:221
  80.2 2.9 %collective-permute-done.15 = bf16[64,192]{1,0:T(8,128)(2,1)S(1)} collective-permute-done((bf16[64,192]{1,0:T(8,128)(2,1)S(1)}, bf16[64,192]{1,0:T(8,128)(2,1)S(1)}, u32[]{:S(2)}, u32[]{:S(2)}) %collective-permute-start.15) | collective-permute-done | bytes 24608 | tf_op jit(solution)/shard_map/ppermute | solution.py:221
  83.5 1.6 %collective-permute-start.16 = (bf16[1,12288]{1,0:T(2,128)(2,1)S(1)}, bf16[1,12288]{1,0:T(2,128)(2,1)S(1)}, u32[]{:S(2)}, u32[]{:S(2)}) collective-permute-start(bf16[1,12288]{1,0:T(2,128)(2,1)S(1)} %constant_dynamic-update-slice_fusion.refs_0_), channel_id=1, source_target_pairs={{0,1},{1,0},{2,3},{3,2},{4,5},{5,4},{6,7},{7,6},{8,9},{9,8},{10,11... | collective-permute-start | bytes 73736 | tf_op jit(solution)/shard_map/ppermute | solution.py:221
  85.1 0.5 collective-permute-start.17
  85.6 1.5 %collective-permute-start.18 = (bf16[1,12288]{1,0:T(2,128)(2,1)S(1)}, bf16[1,12288]{1,0:T(2,128)(2,1)S(1)}, u32[]{:S(2)}, u32[]{:S(2)}) collective-permute-start(bf16[1,12288]{1,0:T(2,128)(2,1)S(1)} %constant_dynamic-update-slice_fusion.refs_0_), channel_id=1, source_target_pairs={{0,3},{1,2},{2,1},{3,0},{4,7},{5,6},{6,5},{7,4},{8,11},{9,10},{10,... | collective-permute-start | bytes 73736 | tf_op jit(solution)/shard_map/ppermute | solution.py:221
  87.1 1.0 %collective-permute-done.16.refs_1_ = bf16[1,12288]{1,0:T(2,128)(2,1)S(1)} collective-permute-done((bf16[1,12288]{1,0:T(2,128)(2,1)S(1)}, bf16[1,12288]{1,0:T(2,128)(2,1)S(1)}, u32[]{:S(2)}, u32[]{:S(2)}) %collective-permute-start.16) | collective-permute-done | bytes 24608 | tf_op jit(solution)/shard_map/ppermute | solution.py:221
  88.1 1.1 %collective-permute-done.17.refs_2_ = bf16[1,12288]{1,0:T(2,128)(2,1)S(1)} collective-permute-done((bf16[1,12288]{1,0:T(2,128)(2,1)S(1)}, bf16[1,12288]{1,0:T(2,128)(2,1)S(1)}, u32[]{:S(2)}, u32[]{:S(2)}) %collective-permute-start.17) | collective-permute-done | bytes 24608 | tf_op jit(solution)/shard_map/ppermute | solution.py:221
  89.2 1.4 %collective-permute-done.18.refs_3_ = bf16[1,12288]{1,0:T(2,128)(2,1)S(1)} collective-permute-done((bf16[1,12288]{1,0:T(2,128)(2,1)S(1)}, bf16[1,12288]{1,0:T(2,128)(2,1)S(1)}, u32[]{:S(2)}, u32[]{:S(2)}) %collective-permute-start.18) | collective-permute-done | bytes 24608 | tf_op jit(solution)/shard_map/ppermute | solution.py:221
  90.6 1.7 %score.1 = f32[4,128]{1,0:T(4,128)} custom-call(s32[1]{0:T(128)} %bitcast.e_ref, bf16[1,12288]{1,0:T(2,128)(2,1)S(1)} %constant_dynamic-update-slice_fusion.refs_0_, bf16[1,12288]{1,0:T(2,128)(2,1)S(1)} %collective-permute-done.16.refs_1_, bf16[1,12288]{1,0:T(2,128)(2,1)S(1)} %collective-permute-done.17.refs_2_, ...), custom_call_target="tpu_custom_call" | custom-call | tf_op jit(solution)/shard_map/score/pallas_call | solution.py:187
  (40 shorter events, 0.9 us)
Async XLA Ops:
  0.0 1.2 %copy-start = (bf16[256,2048]{1,0:T(8,128)(2,1)S(1)}, bf16[256,2048]{1,0:T(8,128)(2,1)}, u32[]{:S(2)}) copy-start(bf16[256,2048]{1,0:T(8,128)(2,1)} %refs_3_.11) | copy-start | bytes 3145732
  1.2 1.2 %copy-start.1 = (bf16[256,2048]{1,0:T(8,128)(2,1)S(1)}, bf16[256,2048]{1,0:T(8,128)(2,1)}, u32[]{:S(2)}) copy-start(bf16[256,2048]{1,0:T(8,128)(2,1)} %refs_7_.11) | copy-start | bytes 3145732
  2.5 5.2 %copy-start.2 = (bf16[2048,3584]{1,0:T(8,128)(2,1)S(1)}, bf16[2048,3584]{1,0:T(8,128)(2,1)}, u32[]{:S(2)}) copy-start(bf16[2048,3584]{1,0:T(8,128)(2,1)} %refs_8_.11) | copy-start | bytes 44040196
  7.6 0.9 %copy-start.7 = (bf16[2048,64]{0,1:T(8,128)(2,1)S(1)}, bf16[2048,64]{0,1:T(8,128)(2,1)}, u32[]{:S(2)}) copy-start(bf16[2048,64]{0,1:T(8,128)(2,1)} %param.17) | copy-start | bytes 786436
  8.6 0.9 %copy-start.8 = (bf16[2048,64]{0,1:T(8,128)(2,1)S(1)}, bf16[2048,64]{0,1:T(8,128)(2,1)}, u32[]{:S(2)}) copy-start(bf16[2048,64]{0,1:T(8,128)(2,1)} %param.21) | copy-start | bytes 786436
  12.8 30.8 %collective-permute-start = (bf16[1,128,896]{2,1,0:T(8,128)(2,1)S(1)}, bf16[1,128,896]{2,1,0:T(8,128)(2,1)S(1)}, u32[]{:S(2)}, u32[]{:S(2)}) collective-permute-start(bf16[1,128,896]{2,1,0:T(8,128)(2,1)S(1)} %get-tuple-element.18), channel_id=1, source_target_pairs={{0,1},{1,0},{2,3},{3,2},{4,5},{5,4},{6,7},{7,6},{8,9},{9,8},{10,11... | collective-permute-start | bytes 688136 | tf_op jit(solution)/shard_map/ppermute | solution.py:221
  19.5 25.8 %collective-permute-start.10 = (bf16[2,128,768]{2,1,0:T(8,128)(2,1)S(1)}, bf16[2,128,768]{2,1,0:T(8,128)(2,1)S(1)}, u32[]{:S(2)}, u32[]{:S(2)}) collective-permute-start(bf16[2,128,768]{2,1,0:T(8,128)(2,1)S(1)} %get-tuple-element.28), channel_id=1, source_target_pairs={{0,2},{1,3},{2,0},{3,1},{4,6},{5,7},{6,4},{7,5},{8,10},{9,11},{10,... | collective-permute-start | bytes 1179656 | tf_op jit(solution)/shard_map/ppermute | solution.py:221
  26.4 19.5 %collective-permute-start.8 = (bf16[3,128,768]{2,1,0:T(8,128)(2,1)S(1)}, bf16[3,128,768]{2,1,0:T(8,128)(2,1)S(1)}, u32[]{:S(2)}, u32[]{:S(2)}) collective-permute-start(bf16[3,128,768]{2,1,0:T(8,128)(2,1)S(1)} %get-tuple-element.26), channel_id=1, source_target_pairs={{0,1},{1,0},{2,3},{3,2},{4,5},{5,4},{6,7},{7,6},{8,9},{9,8},{10,11... | collective-permute-start | bytes 1769480 | tf_op jit(solution)/shard_map/ppermute | solution.py:221
  32.4 16.1 %collective-permute-start.6 = (bf16[3,128,768]{2,1,0:T(8,128)(2,1)S(1)}, bf16[3,128,768]{2,1,0:T(8,128)(2,1)S(1)}, u32[]{:S(2)}, u32[]{:S(2)}) collective-permute-start(bf16[3,128,768]{2,1,0:T(8,128)(2,1)S(1)} %get-tuple-element.24), channel_id=1, source_target_pairs={{0,2},{1,3},{2,0},{3,1},{4,6},{5,7},{6,4},{7,5},{8,10},{9,11},{10,... | collective-permute-start | bytes 1769480 | tf_op jit(solution)/shard_map/ppermute | solution.py:221
  37.9 23.3 %copy-start.3 = (bf16[3584,64]{0,1:T(8,128)(2,1)S(1)}, bf16[3584,64]{0,1:T(8,128)(2,1)}, u32[]{:S(2)}) copy-start(bf16[3584,64]{0,1:T(8,128)(2,1)} %param.18) | copy-start | bytes 1376260
  37.9 23.2 %copy-start.4 = (bf16[3584,64]{0,1:T(8,128)(2,1)S(1)}, bf16[3584,64]{0,1:T(8,128)(2,1)}, u32[]{:S(2)}) copy-start(bf16[3584,64]{0,1:T(8,128)(2,1)} %param.19) | copy-start | bytes 1376260
  37.9 23.2 %copy-start.5 = (bf16[3584,64]{0,1:T(8,128)(2,1)S(1)}, bf16[3584,64]{0,1:T(8,128)(2,1)}, u32[]{:S(2)}) copy-start(bf16[3584,64]{0,1:T(8,128)(2,1)} %param.20) | copy-start | bytes 1376260
  37.9 17.2 %collective-permute-start.4 = (bf16[3,128,768]{2,1,0:T(8,128)(2,1)S(1)}, bf16[3,128,768]{2,1,0:T(8,128)(2,1)S(1)}, u32[]{:S(2)}, u32[]{:S(2)}) collective-permute-start(bf16[3,128,768]{2,1,0:T(8,128)(2,1)S(1)} %get-tuple-element.22), channel_id=1, source_target_pairs={{0,1},{1,0},{2,3},{3,2},{4,5},{5,4},{6,7},{7,6},{8,9},{9,8},{10,11... | collective-permute-start | bytes 1769480 | tf_op jit(solution)/shard_map/ppermute | solution.py:221
  43.6 46.9 %copy-start.6 = (bf16[128,12288]{1,0:T(8,128)(2,1)S(1)}, bf16[128,12288]{1,0:T(8,128)(2,1)}, u32[]{:S(2)}) copy-start(bf16[128,12288]{1,0:T(8,128)(2,1)} %refs_4_.13) | copy-start | bytes 9437188
  43.6 46.9 %copy-start.9 = (s32[1,128]{1,0:T(1,128)S(1)}, s32[1,128]{1,0:T(1,128)}, u32[]{:S(2)}) copy-start(s32[1,128]{1,0:T(1,128)} %refs_5_.13) | copy-start | bytes 1540
  43.7 13.3 %collective-permute-start.2 = (bf16[2,128,768]{2,1,0:T(8,128)(2,1)S(1)}, bf16[2,128,768]{2,1,0:T(8,128)(2,1)S(1)}, u32[]{:S(2)}, u32[]{:S(2)}) collective-permute-start(bf16[2,128,768]{2,1,0:T(8,128)(2,1)S(1)} %get-tuple-element.20), channel_id=1, source_target_pairs={{0,2},{1,3},{2,0},{3,1},{4,6},{5,7},{6,4},{7,5},{8,10},{9,11},{10,... | collective-permute-start | bytes 1179656 | tf_op jit(solution)/shard_map/ppermute | solution.py:221
  45.3 14.1 %collective-permute-start.1 = (bf16[1,64,896]{2,1,0:T(8,128)(2,1)S(1)}, bf16[1,64,896]{2,1,0:T(8,128)(2,1)S(1)}, u32[]{:S(2)}, u32[]{:S(2)}) collective-permute-start(bf16[1,64,896]{2,1,0:T(8,128)(2,1)S(1)} %add_convert_fusion.5), channel_id=1, source_target_pairs={{0,2},{1,3},{2,0},{3,1},{4,6},{5,7},{6,4},{7,5},{8,10},{9,11},{10,... | collective-permute-start | bytes 344072 | tf_op jit(solution)/shard_map/ppermute | solution.py:221
  45.9 15.4 %collective-permute-start.11 = (bf16[2,64,768]{2,1,0:T(8,128)(2,1)S(1)}, bf16[2,64,768]{2,1,0:T(8,128)(2,1)S(1)}, u32[]{:S(2)}, u32[]{:S(2)}) collective-permute-start(bf16[2,64,768]{2,1,0:T(8,128)(2,1)S(1)} %add_convert_fusion.3), channel_id=1, source_target_pairs={{0,1},{1,0},{2,3},{3,2},{4,5},{5,4},{6,7},{7,6},{8,9},{9,8},{10,11... | collective-permute-start | bytes 589832 | tf_op jit(solution)/shard_map/ppermute | solution.py:221
  48.5 17.2 %collective-permute-start.9 = (bf16[3,64,768]{2,1,0:T(8,128)(2,1)S(1)}, bf16[3,64,768]{2,1,0:T(8,128)(2,1)S(1)}, u32[]{:S(2)}, u32[]{:S(2)}) collective-permute-start(bf16[3,64,768]{2,1,0:T(8,128)(2,1)S(1)} %add_convert_fusion), channel_id=1, source_target_pairs={{0,2},{1,3},{2,0},{3,1},{4,6},{5,7},{6,4},{7,5},{8,10},{9,11},{10,... | collective-permute-start | bytes 884744 | tf_op jit(solution)/shard_map/ppermute | solution.py:221
  55.1 11.5 %collective-permute-start.7 = (bf16[3,64,768]{2,1,0:T(8,128)(2,1)S(1)}, bf16[3,64,768]{2,1,0:T(8,128)(2,1)S(1)}, u32[]{:S(2)}, u32[]{:S(2)}) collective-permute-start(bf16[3,64,768]{2,1,0:T(8,128)(2,1)S(1)} %add_convert_fusion.1), channel_id=1, source_target_pairs={{0,1},{1,0},{2,3},{3,2},{4,5},{5,4},{6,7},{7,6},{8,9},{9,8},{10,11... | collective-permute-start | bytes 884744 | tf_op jit(solution)/shard_map/ppermute | solution.py:221
  57.0 13.2 %collective-permute-start.5 = (bf16[3,64,768]{2,1,0:T(8,128)(2,1)S(1)}, bf16[3,64,768]{2,1,0:T(8,128)(2,1)S(1)}, u32[]{:S(2)}, u32[]{:S(2)}) collective-permute-start(bf16[3,64,768]{2,1,0:T(8,128)(2,1)S(1)} %add_convert_fusion.2), channel_id=1, source_target_pairs={{0,2},{1,3},{2,0},{3,1},{4,6},{5,7},{6,4},{7,5},{8,10},{9,11},{10,... | collective-permute-start | bytes 884744 | tf_op jit(solution)/shard_map/ppermute | solution.py:221
  59.4 11.6 %collective-permute-start.3 = (bf16[2,64,768]{2,1,0:T(8,128)(2,1)S(1)}, bf16[2,64,768]{2,1,0:T(8,128)(2,1)S(1)}, u32[]{:S(2)}, u32[]{:S(2)}) collective-permute-start(bf16[2,64,768]{2,1,0:T(8,128)(2,1)S(1)} %add_convert_fusion.4), channel_id=1, source_target_pairs={{0,1},{1,0},{2,3},{3,2},{4,5},{5,4},{6,7},{7,6},{8,9},{9,8},{10,11... | collective-permute-start | bytes 589832 | tf_op jit(solution)/shard_map/ppermute | solution.py:221
  71.8 1.3 %collective-permute-start.12 = (bf16[64,192]{1,0:T(8,128)(2,1)S(1)}, bf16[64,192]{1,0:T(8,128)(2,1)S(1)}, u32[]{:S(2)}, u32[]{:S(2)}) collective-permute-start(bf16[64,192]{1,0:T(8,128)(2,1)S(1)} %outer.1), channel_id=1, source_target_pairs={{0,4},{4,0},{8,12},{12,8},{16,20},{20,16},{24,28},{28,24},{1,5},{5... | collective-permute-start | bytes 73736 | tf_op jit(solution)/shard_map/ppermute | solution.py:221
  73.1 4.5 %collective-permute-start.13 = (bf16[64,192]{1,0:T(8,128)(2,1)S(1)}, bf16[64,192]{1,0:T(8,128)(2,1)S(1)}, u32[]{:S(2)}, u32[]{:S(2)}) collective-permute-start(bf16[64,192]{1,0:T(8,128)(2,1)S(1)} %add_convert_fusion.7), channel_id=1, source_target_pairs={{0,8},{4,12},{8,0},{12,4},{16,24},{20,28},{24,16},{28,20},{1,9},{5... | collective-permute-start | bytes 73736 | tf_op jit(solution)/shard_map/ppermute | solution.py:221
  74.8 5.4 %collective-permute-start.14 = (bf16[64,192]{1,0:T(8,128)(2,1)S(1)}, bf16[64,192]{1,0:T(8,128)(2,1)S(1)}, u32[]{:S(2)}, u32[]{:S(2)}) collective-permute-start(bf16[64,192]{1,0:T(8,128)(2,1)S(1)} %add_convert_fusion.7), channel_id=1, source_target_pairs={{0,16},{4,20},{8,24},{12,28},{16,0},{20,4},{24,8},{28,12},{1,17},{... | collective-permute-start | bytes 73736 | tf_op jit(solution)/shard_map/ppermute | solution.py:221
  77.3 5.7 %collective-permute-start.15 = (bf16[64,192]{1,0:T(8,128)(2,1)S(1)}, bf16[64,192]{1,0:T(8,128)(2,1)S(1)}, u32[]{:S(2)}, u32[]{:S(2)}) collective-permute-start(bf16[64,192]{1,0:T(8,128)(2,1)S(1)} %add_convert_fusion.7), channel_id=1, source_target_pairs={{0,24},{4,28},{8,16},{12,20},{16,8},{20,12},{24,0},{28,4},{1,25},{... | collective-permute-start | bytes 73736 | tf_op jit(solution)/shard_map/ppermute | solution.py:221
  83.5 4.6 %collective-permute-start.16 = (bf16[1,12288]{1,0:T(2,128)(2,1)S(1)}, bf16[1,12288]{1,0:T(2,128)(2,1)S(1)}, u32[]{:S(2)}, u32[]{:S(2)}) collective-permute-start(bf16[1,12288]{1,0:T(2,128)(2,1)S(1)} %constant_dynamic-update-slice_fusion.refs_0_), channel_id=1, source_target_pairs={{0,1},{1,0},{2,3},{3,2},{4,5},{5,4},{6,7},{7,6},{8,9},{9,8},{10,11... | collective-permute-start | bytes 73736 | tf_op jit(solution)/shard_map/ppermute | solution.py:221
  85.1 4.1 %collective-permute-start.17 = (bf16[1,12288]{1,0:T(2,128)(2,1)S(1)}, bf16[1,12288]{1,0:T(2,128)(2,1)S(1)}, u32[]{:S(2)}, u32[]{:S(2)}) collective-permute-start(bf16[1,12288]{1,0:T(2,128)(2,1)S(1)} %constant_dynamic-update-slice_fusion.refs_0_), channel_id=1, source_target_pairs={{0,2},{1,3},{2,0},{3,1},{4,6},{5,7},{6,4},{7,5},{8,10},{9,11},{10,... | collective-permute-start | bytes 73736 | tf_op jit(solution)/shard_map/ppermute | solution.py:221
  85.6 5.0 %collective-permute-start.18 = (bf16[1,12288]{1,0:T(2,128)(2,1)S(1)}, bf16[1,12288]{1,0:T(2,128)(2,1)S(1)}, u32[]{:S(2)}, u32[]{:S(2)}) collective-permute-start(bf16[1,12288]{1,0:T(2,128)(2,1)S(1)} %constant_dynamic-update-slice_fusion.refs_0_), channel_id=1, source_target_pairs={{0,3},{1,2},{2,1},{3,0},{4,7},{5,6},{6,5},{7,4},{8,11},{9,10},{10,... | collective-permute-start | bytes 73736 | tf_op jit(solution)/shard_map/ppermute | solution.py:221

commit v2 on v0

v2 whole, which is shorter than its diff:
```python
import functools

import jax
import jax.numpy as jnp
from jax import lax
from jax.experimental import pallas as pl
from jax.experimental.pallas import tpu as pltpu
from jax.sharding import PartitionSpec as P

SEQ_LEN = 64
PLAN = [([], [], [(2, n % 2)]) for n in range(7)]
NT = (((1,), (1,)), ((), ()))
TN = (((0,), (0,)), ((), ()))
F32 = jnp.float32
BF16 = jnp.bfloat16


def plan_of(total):
    if total == 14:
        return PLAN
    plan = [([], [], [(1, 0)])]
    left = total - 1
    while left:
        n = len(plan)
        back = [n - 3] if n >= 3 else []
        take = [n - 5] if n >= 5 else []
        plan.append((back, take, [(min(2, left), n % 2)]))
        left -= plan[-1][2][0][0]
    return plan


def pieces_of(steps, width):
    pieces = [(2 * width * p, 2 * width) for p in range(steps // 2)]
    if steps % 2:
        pieces.append(((steps - 1) * width, width))
    return pieces


def partials_kernel(count, groups, opening, extra, first, pieces, ahead, waits, *refs):
    refs = list(refs)
    own = refs.pop(0)[0] if opening else None
    acts_in, grads_in, w_gate, w_up, w_down = refs[:5]
    refs = refs[5:]
    held = None if opening else refs.pop(0)
    p_in, p_out = (refs.pop(0), refs.pop(0)) if extra else (None, None)
    refs = refs[waits:]
    outs = [(refs.pop(0), refs.pop(0)) for _ in groups]
    acts, grads = (refs.pop(0), refs.pop(0)) if opening else (acts_in, grads_in)
    later = refs.pop(0) if ahead else None
    sems = refs.pop()
    gates = [refs.pop(0) if opening or n else held for n in range(len(pieces))]
    ups = [refs.pop(0) for _ in pieces]
    downs = [refs.pop(0) for _ in pieces]

    used = []

    def copy(source, target):
        job = pltpu.make_async_copy(source, target, sems.at[len(used)])
        job.start()
        used.append(job)
        return job

    def reorder(source, target):
        if not opening:
            return []
        return [
            copy(
                source.at[pl.ds(pl.multiple_of((own ^ j) * SEQ_LEN, SEQ_LEN), SEQ_LEN), :],
                target.at[pl.ds(j * SEQ_LEN, SEQ_LEN), :],
            )
            for j in range(count)
        ]

    wait_acts = reorder(acts_in, acts)
    wait_grads = []
    loads = []
    for number, (at, columns) in enumerate(pieces):
        hidden = pl.ds(first + at, columns)
        jobs = []
        jobs.append(copy(w_gate.at[:, hidden], gates[number]) if opening or number else None)
        jobs.append(copy(w_up.at[:, hidden], ups[number]))
        if number == 0:
            wait_grads = reorder(grads_in, grads)
        jobs.append(copy(w_down.at[hidden, :], downs[number]))
        loads.append(jobs)
    if ahead:
        at, columns = ahead
        next_load = copy(w_gate.at[:, pl.ds(at, columns)], later)

    def place(group, at, value):
        filled = [0, 0]
        for j in range(count):
            stays = 0 if j & groups[group][0] else 1
            rows = pl.ds(filled[stays] * SEQ_LEN, SEQ_LEN)
            outs[group][stays][rows, at : at + value.shape[1]] = value[
                j * SEQ_LEN : (j + 1) * SEQ_LEN
            ]
            filled[stays] += 1

    def put(kind, at, part):
        value = part.astype(BF16)
        for group, (_, begin, end) in enumerate(groups):
            low, high = max(at, begin), min(at + value.shape[1], end)
            if low < high:
                place(group, kind * (end - begin) + low - begin, value[:, low - at : high - at])

    for job in wait_acts:
        job.wait()
    for number, (at, columns) in enumerate(pieces):
        gate, up, back = loads[number]
        if gate is not None:
            gate.wait()
        put(0, at, jnp.dot(acts[...], gates[number][...], preferred_element_type=F32))
        if number == 0 and extra:
            place(
                0,
                3 * (groups[0][2] - groups[0][1]),
                jnp.concatenate(
                    [
                        lax.dot_general(acts[...], p_in[...], NT, preferred_element_type=F32),
                        lax.dot_general(grads[...], p_out[...], NT, preferred_element_type=F32),
                    ],
                    axis=1,
                ).astype(BF16),
            )
        up.wait()
        put(1, at, jnp.dot(acts[...], ups[number][...], preferred_element_type=F32))
        if number == 0:
            for job in wait_grads:
                job.wait()
        back.wait()
        put(
            2,
            at,
            lax.dot_general(grads[...], downs[number][...], NT, preferred_element_type=F32),
        )
    if ahead:
        next_load.wait()


def partials(
    own, acts, grads, w_gate, w_up, w_down, held, extras, after, first, pieces, ahead, groups, opening
):
    tokens, depth = acts.shape
    count = tokens // SEQ_LEN
    whole = sum(columns for _, columns in pieces)
    columns = 3 * whole + sum(x.shape[0] for x in extras)
    hbm = pl.BlockSpec(memory_space=pltpu.HBM)
    vmem = pl.BlockSpec(memory_space=pltpu.VMEM)
    anywhere = pl.BlockSpec(memory_space=pl.ANY)
    shapes = []
    for number, (_, begin, end) in enumerate(groups):
        own_columns = 3 * (end - begin) + (0 if number else sum(x.shape[0] for x in extras))
        shapes += [jax.ShapeDtypeStruct((count // 2 * SEQ_LEN, own_columns), BF16)] * 2
    if opening:
        shapes += [jax.ShapeDtypeStruct(acts.shape, BF16)] * 2
    if ahead:
        shapes.append(jax.ShapeDtypeStruct((depth, ahead[1]), BF16))
    rows = hbm if opening else vmem
    wide = [pltpu.VMEM((depth, c), BF16) for _, c in pieces]
    scratch = (wide if opening else wide[1:]) + wide + [
        pltpu.VMEM((c, depth), BF16) for _, c in pieces
    ]
    copies = 3 * len(pieces) + (2 * count if opening else -1) + (1 if ahead else 0)
    return pl.pallas_call(
        functools.partial(
            partials_kernel,
            count,
            groups,
            opening,
            len(extras) > 0,
            first,
            pieces,
            ahead,
            len(after),
        ),
        out_shape=shapes,
        in_specs=([pl.BlockSpec(memory_space=pltpu.SMEM)] if opening else [])
        + [rows, rows, hbm, hbm, hbm]
        + ([] if opening else [vmem])
        + [vmem] * len(extras)
        + [anywhere] * len(after),
        out_specs=[vmem] * len(shapes),
        scratch_shapes=scratch + [pltpu.SemaphoreType.DMA((copies,))],
        compiler_params=pltpu.CompilerParams(vmem_limit_bytes=32 << 20),
        cost_estimate=pl.CostEstimate(
            flops=2 * tokens * depth * columns,
            bytes_accessed=6 * depth * whole + 2 * tokens * columns,
            transcendentals=0,
        ),
        name=f"partials_{first}",
    )(
        *([own] if opening else []),
        acts,
        grads,
        w_gate,
        w_up,
        w_down,
        *([] if opening else [held]),
        *extras,
        *after,
    )


def project_kernel(terms, pieces, first, rank, sums, *refs):
    addends, refs = refs[:terms], refs[terms:]
    p_gate, p_up, p_hidden = refs[:3]
    refs = refs[3:]
    before = refs[0]
    out = refs[-1]
    whole = sum(columns for _, columns in pieces)

    def total(refs, at, columns):
        return functools.reduce(
            jnp.add, [r[:SEQ_LEN, at : at + columns].astype(F32) for r in refs]
        )

    part = before[...]
    for start, columns in pieces:
        gate = total(addends, start, columns)
        up = total(addends, whole + start, columns)
        back = total(addends, 2 * whole + start, columns)
        sig = jax.nn.sigmoid(gate)
        gs = gate * sig
        hidden = (gs * up).astype(BF16)
        grad_up = (back * gs).astype(BF16)
        grad_gate = (back * up * sig * (1.0 + gate * (1.0 - sig))).astype(BF16)
        units = slice(first + start, first + start + columns)
        part = part + jnp.concatenate(
            [
                lax.dot_general(value, weights[:, units], NT, preferred_element_type=F32)
                for value, weights in ((grad_gate, p_gate), (grad_up, p_up), (hidden, p_hidden))
            ],
            axis=1,
        )
    if sums is None:
        out[...] = part
        return
    number, at = sums
    both = total(refs[1 : 1 + number], at, 2 * rank)

    def outer(a, b):
        return lax.dot_general(
            a, b, TN, preferred_element_type=F32, precision=lax.Precision.HIGHEST
        )

    out[:, : 2 * rank] = outer(both[:, :rank], part[:, : 2 * rank]).astype(BF16)
    out[:, 2 * rank :] = outer(part[:, 2 * rank :], both[:, rank:]).astype(BF16)


def project(addends, projections, before, first, pieces, sums=(), at=0):
    rank = projections[0].shape[0]
    vmem = pl.BlockSpec(memory_space=pltpu.VMEM)
    shape = (
        jax.ShapeDtypeStruct((rank, 3 * rank), BF16)
        if sums
        else jax.ShapeDtypeStruct(before.shape, F32)
    )
    return pl.pallas_call(
        functools.partial(
            project_kernel,
            len(addends),
            pieces,
            first,
            rank,
            (len(sums), at) if sums else None,
        ),
        out_shape=shape,
        in_specs=[vmem] * (len(addends) + 4 + len(sums)),
        out_specs=vmem,
        compiler_params=pltpu.CompilerParams(vmem_limit_bytes=16 << 20),
        cost_estimate=pl.CostEstimate(
            flops=6 * SEQ_LEN * rank * sum(c for _, c in pieces),
            bytes_accessed=2 * addends[0].size,
            transcendentals=SEQ_LEN * sum(c for _, c in pieces),
        ),
        name=f"project_{first}",
    )(*addends, *projections, before, *sums)


def score_kernel(count, e_ref, *refs):
    queries, (store, ids, out, rows) = refs[:count], refs[count:]
    for j in range(count):
        rows[pl.ds(e_ref[0] ^ j, 1), :] = queries[j][...].astype(F32)
    lhs = rows[...].astype(BF16)
    natural = lax.dot_general(lhs, store[...], NT, preferred_element_type=F32)
    docs = store.shape[0]
    chosen = lax.broadcasted_iota(jnp.int32, (docs, docs), 0) == ids[...]
    out[...] = jnp.dot(
        natural, chosen.astype(F32), preferred_element_type=F32, precision=lax.Precision.HIGHEST
    )


def score(index, queries, store, ids):
    count = len(queries)
    docs, size = store.shape
    vmem = pl.BlockSpec(memory_space=pltpu.VMEM)
    return pl.pallas_call(
        functools.partial(score_kernel, count),
        out_shape=jax.ShapeDtypeStruct((count, docs), F32),
        in_specs=[pl.BlockSpec(memory_space=pltpu.SMEM)] + [vmem] * (count + 2),
        out_specs=vmem,
        scratch_shapes=[pltpu.VMEM((count, size), F32)],
        compiler_params=pltpu.CompilerParams(vmem_limit_bytes=16 << 20),
        name="score",
    )(index, *queries, store, ids)


def local(
    mesh_sizes,
    acts,
    out_grad,
    w_gate,
    w_up,
    w_down,
    proj_in,
    proj_gate,
    proj_up,
    proj_hidden,
    proj_out,
    store,
    doc_ids,
):
    tensor, example = mesh_sizes
    units = w_gate.shape[1]
    rank = proj_in.shape[1]
    width = 256 if units % 256 == 0 else 128
    index = lax.axis_index("example").astype(jnp.int32).reshape(1)

    def flip(x, axis, k):
        n = tensor if axis == "tensor" else example
        return lax.ppermute(x, axis, [(i, i ^ k) for i in range(n)])

    bits = [1 << b for b in range(example.bit_length() - 1)]
    extras = (proj_in.T, proj_out.T)
    projections = (proj_gate.T, proj_up.T, proj_hidden.T)

    def rows_of(x, blocks, chosen):
        return jnp.concatenate(
            [x[i * SEQ_LEN : (i + 1) * SEQ_LEN] for i, j in enumerate(blocks) if j in chosen],
            axis=0,
        )

    def summed(addends, blocks, chosen):
        return functools.reduce(
            jnp.add, [rows_of(x, blocks, chosen).astype(F32) for x in addends]
        ).astype(BF16)

    def later_stages(addends, order):
        blocks = [j for j in range(example) if not j & order[0]]
        sent = None
        for bit in order[1:]:
            stay = [j for j in blocks if not j & bit]
            send = summed(addends, blocks, [j for j in blocks if j & bit])
            sent = send if sent is None else sent
            if len(stay) > 1:
                addends = [summed(addends, blocks, stay)]
            addends = addends + [flip(send, "example", bit)]
            blocks = stay
        return addends, sent

    acts, out_grad, w_gate, w_up, w_down = (
        pltpu.with_memory_space_constraint(x, pltpu.HBM)
        for x in (acts, out_grad, w_gate, w_up, w_down)
    )
    plan = plan_of(units // width)
    sizes = [(steps * width, side) for _, _, call in plan for steps, side in call]
    firsts = [sum(size for size, _ in sizes[:n]) for n in range(len(sizes))]
    calls = []
    for _, _, call in plan:
        start = sum(len(c) for c in calls)
        calls.append(list(range(start, start + len(call))))
    widths = [sum(sizes[n][0] for n in call) for call in calls]
    holder = calls[min(2, len(calls) - 1)][0]
    acts_rows, grads_rows = acts, out_grad
    begun, done = [], []
    part = jnp.zeros((SEQ_LEN, 3 * rank), F32)
    sent, held, taken = None, None, 0

    def turn_back(number):
        addends, order = begun[number]
        addends, onward = later_stages(addends, order)
        done.append(addends)
        return [] if onward is None else [onward]

    def take_in(number, part):
        return project(
            done[number],
            projections,
            part,
            firsts[number],
            pieces_of(sizes[number][0] // width, width),
            *((done[holder], 3 * sizes[holder][0]) if number == len(sizes) - 1 else ()),
        )

    for index_of, (back, take, _) in enumerate(plan):
        call = calls[index_of]
        after = [] if sent is None or index_of == 0 else [sent]
        for number in back:
            after = after + turn_back(number)
        for number in take:
            part = take_in(number, part)
            after = after + [part]
            taken += 1
        first = firsts[call[0]]
        ahead = None
        if index_of + 1 < len(plan):
            ahead = (first + widths[index_of], pieces_of(widths[index_of + 1] // width, width)[0][1])
        orders = [bits[::-1] if sizes[n][1] else bits for n in call]
        results = partials(
            index,
            acts_rows,
            grads_rows,
            w_gate,
            w_up,
            w_down,
            held,
            extras if call[0] == holder else (),
            after,
            first,
            pieces_of(widths[index_of] // width, width),
            ahead,
            [
                (order[0], firsts[n] - first, firsts[n] - first + sizes[n][0])
                for n, order in zip(call, orders)
            ],
            index_of == 0,
        )
        for order in orders:
            sent, keep, *results = results
            begun.append(([keep, flip(sent, "example", order[0])], order))
        if index_of == 0:
            acts_rows, grads_rows, *results = results
        held = results[0] if ahead else None
    while len(done) < len(sizes):
        turn_back(len(done))
    while taken < len(sizes):
        part = take_in(taken, part)
        taken += 1

    pair = (part.astype(F32) + flip(part, "tensor", 1).astype(F32)).astype(BF16)
    whole = functools.reduce(
        jnp.add, [pair.astype(F32)] + [flip(pair, "tensor", k).astype(F32) for k in range(2, tensor, 2)]
    ).astype(BF16)
    query = jnp.concatenate(
        [whole[:, m * rank : (m + 1) * rank].reshape(1, rank * rank) for m in range(3)], axis=1
    )
    queries = [query] + [flip(query, "example", k) for k in range(1, example)]
    return score(index, queries, store, doc_ids)


def solution(mesh):
    return jax.shard_map(
        functools.partial(local, (mesh.shape["tensor"], mesh.shape["example"])),
        mesh=mesh,
        in_specs=(
            P(None, "example"),
            P(None, "example"),
            P("example", "tensor"),
            P("example", "tensor"),
            P("tensor", "example"),
            P("example", None),
            P("tensor", None),
            P("tensor", None),
            P("tensor", None),
            P("example", None),
            P(("tensor", "example"), None),
            P(("tensor", "example"), None),
        ),
        out_specs=P(None, ("tensor", "example")),
        check_vma=False,
    )
```

time: 194 us -> 78.2 us (0.40)
  waiting for transfers between devices: 62.2 us -> 23.5 us
  blocking collectives: 37.6 us -> 0 us
  matrix products: 32.7 us -> 0 us
  Pallas kernels: 0 us -> 29 us
  other arithmetic: 27.3 us -> 0.37 us
  starting transfers between devices: 0.01 us -> 24.4 us
  local copies, waits for them, and re-layouts: 20.1 us -> 0.45 us
  between operations: 13.5 us -> 0.27 us
    unnamed x2 -> x0, waiting for transfers between devices: 62.2 us -> none
    dot_general x10 -> x0, matrix products: 32.7 us -> none  [the longest x1 14.2 us: local(): forward = jnp.dot(acts, left_weights, preferred_element_type=jnp.float32)]
    pallas_call x0 -> x15, Pallas kernels: none -> 29 us  [the longest x7 25.3 us: partials(): pl.pallas_call(functools.partial(partials_kernel, count, groups, opening,...]
    psum x1 -> x0, blocking collectives: 29 us -> none  [local(): lax.psum(hidden_part.astype(jnp.bfloat16), 'tensor').astype(jnp.float32)]
    concatenate x1 -> x0, other arithmetic: 25.2 us -> none  [local(): jnp.concatenate([forward, backward, outward], axis=1).astype(jnp.bfloat16)]
    ppermute x0 -> x21, starting transfers between devices: none -> 24.4 us  [flip(): return lax.ppermute(x, axis, [(i, i ^ k) for i in range(n)])]
    ppermute x0 -> x21, waiting for transfers between devices: none -> 23.5 us  [flip(): return lax.ppermute(x, axis, [(i, i ^ k) for i in range(n)])]
    unnamed x21 -> x16, local copies, waits for them, and re-layouts: 15.6 us -> 0.08 us
  transfers between devices with their start and end apart: 1 -> 21, of which waited for: 1 -> 12; matrix products, arithmetic and copies ran while one was open for 2% -> 0% of each run, Pallas kernels for 0% -> 29%
where the time goes in v2:
time: 78.2 us; the launch traced here: 78 us
  Pallas kernels  29 us (37%)
  starting transfers between devices  24.4 us (31%)
  waiting for transfers between devices  23.5 us (30%)
    pallas_call x7, Pallas kernels, partials(): pl.pallas_call(functools.partial(partials_kernel, count, groups, opening,...  25.3 us
    ppermute x21, starting transfers between devices, flip(): return lax.ppermute(x, axis, [(i, i ^ k) for i in range(n)])  24.4 us
    ppermute x21, waiting for transfers between devices, flip(): return lax.ppermute(x, axis, [(i, i ^ k) for i in range(n)])  23.5 us
    pallas_call x7, Pallas kernels, project(): pl.pallas_call(functools.partial(project_kernel, len(addends), pieces, fi...  2.04 us
    pallas_call x1, Pallas kernels, score(): pl.pallas_call(functools.partial(score_kernel, count), out_shape=jax.Shap...  1.74 us
  transfers between devices with their start and end apart: 21, of which 12 were waited for; matrix products, arithmetic and copies ran while one was open for 0% of the time, Pallas kernels for 29%

profile of v2, /device:TPU:0, one launch (start us, length us, event | category | flops | bytes accessed | tf_op | source)
XLA Modules:
  0.0 78.0 jit_solution(14463935335268321985)
XLA Ops:
  0.0 4.4 %partials_0.1 = (bf16[128,1536]{1,0:T(8,128)(2,1)S(1)}, bf16[128,1536]{1,0:T(8,128)(2,1)S(1)}, bf16[256,2048]{1,0:T(8,128)(2,1)S(1)}, bf16[256,2048]{1,0:T(8,128)(2,1)S(1)}, bf16[2048,512]{1,0:T(8,128)(2,1)S(1)}) custom-call(s32[1]{0:T(128)} %bitcast.refs_0_.e_ref, bf16[256,2048]{1,0:T(8,128)(2,1)} %refs_1_.1, bf16[256,2048]{1,0:T(8,128)(2,1)} %refs_2_.7, ...), custom_call_target="tpu_custom_call" | custom-call | flops 1610612736 | bytes 7077888 | tf_op jit(solution)/shard_map/partials_0/pallas_call | solution.py:165
  4.4 3.0 %collective-permute-start.12 = (bf16[128,1536]{1,0:T(8,128)(2,1)S(1)}, bf16[128,1536]{1,0:T(8,128)(2,1)S(1)}, u32[]{:S(2)}, u32[]{:S(2)}) collective-permute-start(bf16[128,1536]{1,0:T(8,128)(2,1)S(1)} %get-tuple-element.30.refs_6_), channel_id=1, source_target_pairs={{0,1},{1,0},{2,3},{3,2},{4,5},{5,4},{6,7},{7,6},{8,9},{9,8},{10,11... | collective-permute-start | bytes 1179656 | tf_op jit(solution)/shard_map/ppermute | solution.py:332
  7.4 3.6 %partials_512.1 = (bf16[128,1536]{1,0:T(8,128)(2,1)S(1)}, bf16[128,1536]{1,0:T(8,128)(2,1)S(1)}, bf16[2048,512]{1,0:T(8,128)(2,1)S(1)}) custom-call(bf16[256,2048]{1,0:T(8,128)(2,1)S(1)} %get-tuple-element.27.refs_0_, bf16[256,2048]{1,0:T(8,128)(2,1)S(1)} %get-tuple-element.28.refs_1_, bf16[2048,3584]{1,0:T(8,128)(2,1)} %refs_2_.13, ...), custom_call_target="tpu_custom_call" | custom-call | flops 1610612736 | bytes 7077888 | tf_op jit(solution)/shard_map/partials_512/pallas_call | solution.py:165
  11.0 1.6 %collective-permute-start.10 = (bf16[128,1536]{1,0:T(8,128)(2,1)S(1)}, bf16[128,1536]{1,0:T(8,128)(2,1)S(1)}, u32[]{:S(2)}, u32[]{:S(2)}) collective-permute-start(bf16[128,1536]{1,0:T(8,128)(2,1)S(1)} %get-tuple-element.32.refs_8_), channel_id=1, source_target_pairs={{0,2},{1,3},{2,0},{3,1},{4,6},{5,7},{6,4},{7,5},{8,10},{9,11},{10,... | collective-permute-start | bytes 1179656 | tf_op jit(solution)/shard_map/ppermute | solution.py:332
  12.6 3.6 %partials_1024.1 = (bf16[128,1664]{1,0:T(8,128)(2,1)S(1)}, bf16[128,1664]{1,0:T(8,128)(2,1)S(1)}, bf16[2048,512]{1,0:T(8,128)(2,1)S(1)}) custom-call(bf16[256,2048]{1,0:T(8,128)(2,1)S(1)} %get-tuple-element.27.refs_0_, bf16[256,2048]{1,0:T(8,128)(2,1)S(1)} %get-tuple-element.28.refs_1_, bf16[2048,3584]{1,0:T(8,128)(2,1)} %refs_2_.13, ...), custom_call_target="tpu_custom_call" | custom-call | flops 1744830464 | bytes 7143424 | tf_op jit(solution)/shard_map/partials_1024/pallas_call | solution.py:165
  16.2 0.6 collective-permute-start.8
  16.8 3.5 %partials_1536.1 = (bf16[128,1536]{1,0:T(8,128)(2,1)S(1)}, bf16[128,1536]{1,0:T(8,128)(2,1)S(1)}, bf16[2048,512]{1,0:T(8,128)(2,1)S(1)}) custom-call(bf16[256,2048]{1,0:T(8,128)(2,1)S(1)} %get-tuple-element.27.refs_0_, bf16[256,2048]{1,0:T(8,128)(2,1)S(1)} %get-tuple-element.28.refs_1_, bf16[2048,3584]{1,0:T(8,128)(2,1)} %refs_2_.13, ...), custom_call_target="tpu_custom_call" | custom-call | flops 1610612736 | bytes 7077888 | tf_op jit(solution)/shard_map/partials_1536/pallas_call | solution.py:165
  20.3 0.1 collective-permute-start.6
  20.4 3.5 %partials_2048.1 = (bf16[128,1536]{1,0:T(8,128)(2,1)S(1)}, bf16[128,1536]{1,0:T(8,128)(2,1)S(1)}, bf16[2048,512]{1,0:T(8,128)(2,1)S(1)}) custom-call(bf16[256,2048]{1,0:T(8,128)(2,1)S(1)} %get-tuple-element.27.refs_0_, bf16[256,2048]{1,0:T(8,128)(2,1)S(1)} %get-tuple-element.28.refs_1_, bf16[2048,3584]{1,0:T(8,128)(2,1)} %refs_2_.13, ...), custom_call_target="tpu_custom_call" | custom-call | flops 1610612736 | bytes 7077888 | tf_op jit(solution)/shard_map/partials_2048/pallas_call | solution.py:165
  24.0 2.0 %collective-permute-start.4 = (bf16[128,1536]{1,0:T(8,128)(2,1)S(1)}, bf16[128,1536]{1,0:T(8,128)(2,1)S(1)}, u32[]{:S(2)}, u32[]{:S(2)}) collective-permute-start(bf16[128,1536]{1,0:T(8,128)(2,1)S(1)} %get-tuple-element.38.refs_6_), channel_id=1, source_target_pairs={{0,1},{1,0},{2,3},{3,2},{4,5},{5,4},{6,7},{7,6},{8,9},{9,8},{10,11... | collective-permute-start | bytes 1179656 | tf_op jit(solution)/shard_map/ppermute | solution.py:332
  26.0 3.5 %partials_2560.1 = (bf16[128,1536]{1,0:T(8,128)(2,1)S(1)}, bf16[128,1536]{1,0:T(8,128)(2,1)S(1)}, bf16[2048,512]{1,0:T(8,128)(2,1)S(1)}) custom-call(bf16[256,2048]{1,0:T(8,128)(2,1)S(1)} %get-tuple-element.27.refs_0_, bf16[256,2048]{1,0:T(8,128)(2,1)S(1)} %get-tuple-element.28.refs_1_, bf16[2048,3584]{1,0:T(8,128)(2,1)} %refs_2_.13, ...), custom_call_target="tpu_custom_call" | custom-call | flops 1610612736 | bytes 7077888 | tf_op jit(solution)/shard_map/partials_2560/pallas_call | solution.py:165
  29.6 3.1 %partials_3072.1 = (bf16[128,1536]{1,0:T(8,128)(2,1)S(1)}, bf16[128,1536]{1,0:T(8,128)(2,1)S(1)}) custom-call(bf16[256,2048]{1,0:T(8,128)(2,1)S(1)} %get-tuple-element.27.refs_0_, bf16[256,2048]{1,0:T(8,128)(2,1)S(1)} %get-tuple-element.28.refs_1_, bf16[2048,3584]{1,0:T(8,128)(2,1)} %refs_2_.13, bf16[2048,3584]{1,0:T(8,128)(2,1)} %refs_3_.13, ...), custom_call_target="tpu_custom_call" | custom-call | flops 1610612736 | bytes 7077888 | tf_op jit(solution)/shard_map/partials_3072/pallas_call | solution.py:165
  32.7 1.6 %collective-permute-start.2 = (bf16[128,1536]{1,0:T(8,128)(2,1)S(1)}, bf16[128,1536]{1,0:T(8,128)(2,1)S(1)}, u32[]{:S(2)}, u32[]{:S(2)}) collective-permute-start(bf16[128,1536]{1,0:T(8,128)(2,1)S(1)} %get-tuple-element.40.refs_6_), channel_id=1, source_target_pairs={{0,2},{1,3},{2,0},{3,1},{4,6},{5,7},{6,4},{7,5},{8,10},{9,11},{10,... | collective-permute-start | bytes 1179656 | tf_op jit(solution)/shard_map/ppermute | solution.py:332
  34.3 0.6 collective-permute-start
  35.0 0.1 collective-permute-start.13
  35.1 1.0 %collective-permute-done.4.refs_1_ = bf16[128,1536]{1,0:T(8,128)(2,1)S(1)} collective-permute-done((bf16[128,1536]{1,0:T(8,128)(2,1)S(1)}, bf16[128,1536]{1,0:T(8,128)(2,1)S(1)}, u32[]{:S(2)}, u32[]{:S(2)}) %collective-permute-start.4) | collective-permute-done | bytes 393248 | tf_op jit(solution)/shard_map/ppermute | solution.py:332
  36.2 1.0 %collective-permute-start.11 = (bf16[64,1536]{1,0:T(8,128)(2,1)S(1)}, bf16[64,1536]{1,0:T(8,128)(2,1)S(1)}, u32[]{:S(2)}, u32[]{:S(2)}) collective-permute-start(bf16[64,1536]{1,0:T(8,128)(2,1)S(1)} %add_convert_fusion.2), channel_id=1, source_target_pairs={{0,1},{1,0},{2,3},{3,2},{4,5},{5,4},{6,7},{7,6},{8,9},{9,8},{10,11... | collective-permute-start | bytes 589832 | tf_op jit(solution)/shard_map/ppermute | solution.py:332
  37.2 7.6 %collective-permute-done.2.refs_1_ = bf16[128,1536]{1,0:T(8,128)(2,1)S(1)} collective-permute-done((bf16[128,1536]{1,0:T(8,128)(2,1)S(1)}, bf16[128,1536]{1,0:T(8,128)(2,1)S(1)}, u32[]{:S(2)}, u32[]{:S(2)}) %collective-permute-start.2) | collective-permute-done | bytes 393248 | tf_op jit(solution)/shard_map/ppermute | solution.py:332
  44.9 2.1 %collective-permute-start.5 = (bf16[64,1536]{1,0:T(8,128)(2,1)S(1)}, bf16[64,1536]{1,0:T(8,128)(2,1)S(1)}, u32[]{:S(2)}, u32[]{:S(2)}) collective-permute-start(bf16[64,1536]{1,0:T(8,128)(2,1)S(1)} %add_convert_fusion.4), channel_id=1, source_target_pairs={{0,2},{1,3},{2,0},{3,1},{4,6},{5,7},{6,4},{7,5},{8,10},{9,11},{10,... | collective-permute-start | bytes 589832 | tf_op jit(solution)/shard_map/ppermute | solution.py:332
  47.0 1.6 %collective-permute-start.3 = (bf16[64,1536]{1,0:T(8,128)(2,1)S(1)}, bf16[64,1536]{1,0:T(8,128)(2,1)S(1)}, u32[]{:S(2)}, u32[]{:S(2)}) collective-permute-start(bf16[64,1536]{1,0:T(8,128)(2,1)S(1)} %add_convert_fusion.5), channel_id=1, source_target_pairs={{0,1},{1,0},{2,3},{3,2},{4,5},{5,4},{6,7},{7,6},{8,9},{9,8},{10,11... | collective-permute-start | bytes 589832 | tf_op jit(solution)/shard_map/ppermute | solution.py:332
  48.6 0.4 collective-permute-done.13.refs_2_
  49.0 1.5 %collective-permute-start.9 = (bf16[64,1664]{1,0:T(8,128)(2,1)S(1)}, bf16[64,1664]{1,0:T(8,128)(2,1)S(1)}, u32[]{:S(2)}, u32[]{:S(2)}) collective-permute-start(bf16[64,1664]{1,0:T(8,128)(2,1)S(1)} %add_convert_fusion), channel_id=1, source_target_pairs={{0,2},{1,3},{2,0},{3,1},{4,6},{5,7},{6,4},{7,5},{8,10},{9,11},{10,... | collective-permute-start | bytes 638984 | tf_op jit(solution)/shard_map/ppermute | solution.py:332
  50.6 0.1 collective-permute-done.11.refs_2_
  50.6 0.5 collective-permute-start.1
  51.2 0.3 project_0.1.refs_6_
  51.4 0.3 project_512.1.refs_6_
  51.7 5.6 %collective-permute-done.9.refs_2_.refs_9_ = bf16[64,1664]{1,0:T(8,128)(2,1)S(1)} collective-permute-done((bf16[64,1664]{1,0:T(8,128)(2,1)S(1)}, bf16[64,1664]{1,0:T(8,128)(2,1)S(1)}, u32[]{:S(2)}, u32[]{:S(2)}) %collective-permute-start.9) | collective-permute-done | bytes 213024 | tf_op jit(solution)/shard_map/ppermute | solution.py:332
  57.3 0.3 project_1024.1.refs_6_
  57.5 0.3 project_1536.1.refs_6_
  57.8 0.3 project_2048.1.refs_6_
  58.1 0.3 project_2560.1.refs_6_
  58.4 1.0 %collective-permute-done.1.refs_2_ = bf16[64,1536]{1,0:T(8,128)(2,1)S(1)} collective-permute-done((bf16[64,1536]{1,0:T(8,128)(2,1)S(1)}, bf16[64,1536]{1,0:T(8,128)(2,1)S(1)}, u32[]{:S(2)}, u32[]{:S(2)}) %collective-permute-start.1) | collective-permute-done | bytes 196640 | tf_op jit(solution)/shard_map/ppermute | solution.py:332
  59.4 0.5 project_3072.1
  60.0 1.2 %collective-permute-done.14 = bf16[64,192]{1,0:T(8,128)(2,1)S(1)} collective-permute-done((bf16[64,192]{1,0:T(8,128)(2,1)S(1)}, bf16[64,192]{1,0:T(8,128)(2,1)S(1)}, u32[]{:S(2)}, u32[]{:S(2)}) %collective-permute-start.14) | collective-permute-done | bytes 24608 | tf_op jit(solution)/shard_map/ppermute | solution.py:332
  61.2 3.7 %collective-permute-start.17 = (bf16[64,192]{1,0:T(8,128)(2,1)S(1)}, bf16[64,192]{1,0:T(8,128)(2,1)S(1)}, u32[]{:S(2)}, u32[]{:S(2)}) collective-permute-start(bf16[64,192]{1,0:T(8,128)(2,1)S(1)} %add_convert_fusion.8), channel_id=1, source_target_pairs={{0,24},{4,28},{8,16},{12,20},{16,8},{20,12},{24,0},{28,4},{1,25},{... | collective-permute-start | bytes 73736 | tf_op jit(solution)/shard_map/ppermute | solution.py:332
  64.9 0.8 collective-permute-start.15
  65.6 1.3 %collective-permute-done.17 = bf16[64,192]{1,0:T(8,128)(2,1)S(1)} collective-permute-done((bf16[64,192]{1,0:T(8,128)(2,1)S(1)}, bf16[64,192]{1,0:T(8,128)(2,1)S(1)}, u32[]{:S(2)}, u32[]{:S(2)}) %collective-permute-start.17) | collective-permute-done | bytes 24608 | tf_op jit(solution)/shard_map/ppermute | solution.py:332
  67.0 2.7 %collective-permute-done.16 = bf16[64,192]{1,0:T(8,128)(2,1)S(1)} collective-permute-done((bf16[64,192]{1,0:T(8,128)(2,1)S(1)}, bf16[64,192]{1,0:T(8,128)(2,1)S(1)}, u32[]{:S(2)}, u32[]{:S(2)}) %collective-permute-start.16) | collective-permute-done | bytes 24608 | tf_op jit(solution)/shard_map/ppermute | solution.py:332
  69.8 0.1 reshape.15
  69.9 0.1 reshape.14
  70.0 0.1 reshape.13
  70.1 1.5 %collective-permute-start.20 = (bf16[1,12288]{1,0:T(2,128)(2,1)S(1)}, bf16[1,12288]{1,0:T(2,128)(2,1)S(1)}, u32[]{:S(2)}, u32[]{:S(2)}) collective-permute-start(bf16[1,12288]{1,0:T(2,128)(2,1)S(1)} %constant_dynamic-update-slice_fusion.refs_0_), channel_id=1, source_target_pairs={{0,3},{1,2},{2,1},{3,0},{4,7},{5,6},{6,5},{7,4},{8,11},{9,10},{10,... | collective-permute-start | bytes 73736 | tf_op jit(solution)/shard_map/ppermute | solution.py:332
  71.7 0.5 collective-permute-start.19
  72.2 1.5 %collective-permute-start.18 = (bf16[1,12288]{1,0:T(2,128)(2,1)S(1)}, bf16[1,12288]{1,0:T(2,128)(2,1)S(1)}, u32[]{:S(2)}, u32[]{:S(2)}) collective-permute-start(bf16[1,12288]{1,0:T(2,128)(2,1)S(1)} %constant_dynamic-update-slice_fusion.refs_0_), channel_id=1, source_target_pairs={{0,1},{1,0},{2,3},{3,2},{4,5},{5,4},{6,7},{7,6},{8,9},{9,8},{10,11... | collective-permute-start | bytes 73736 | tf_op jit(solution)/shard_map/ppermute | solution.py:332
  73.7 1.6 %collective-permute-done.20.refs_3_ = bf16[1,12288]{1,0:T(2,128)(2,1)S(1)} collective-permute-done((bf16[1,12288]{1,0:T(2,128)(2,1)S(1)}, bf16[1,12288]{1,0:T(2,128)(2,1)S(1)}, u32[]{:S(2)}, u32[]{:S(2)}) %collective-permute-start.20) | collective-permute-done | bytes 24608 | tf_op jit(solution)/shard_map/ppermute | solution.py:332
  75.3 0.5 collective-permute-done.19.refs_2_
  75.8 0.4 collective-permute-done.18.refs_1_
  76.3 1.7 %score.1 = f32[4,128]{1,0:T(4,128)} custom-call(s32[1]{0:T(128)} %bitcast.refs_0_.e_ref, bf16[1,12288]{1,0:T(2,128)(2,1)S(1)} %constant_dynamic-update-slice_fusion.refs_0_, bf16[1,12288]{1,0:T(2,128)(2,1)S(1)} %collective-permute-done.18.refs_1_, bf16[1,12288]{1,0:T(2,128)(2,1)S(1)} %collective-permute-done.19.refs_2_, ...), custom_call_target="tpu_custom_call" | custom-call | tf_op jit(solution)/shard_map/score/pallas_call | solution.py:298
  (40 shorter events, 0.7 us)
Async XLA Ops:
  4.4 28.2 %collective-permute-start.12 = (bf16[128,1536]{1,0:T(8,128)(2,1)S(1)}, bf16[128,1536]{1,0:T(8,128)(2,1)S(1)}, u32[]{:S(2)}, u32[]{:S(2)}) collective-permute-start(bf16[128,1536]{1,0:T(8,128)(2,1)S(1)} %get-tuple-element.30.refs_6_), channel_id=1, source_target_pairs={{0,1},{1,0},{2,3},{3,2},{4,5},{5,4},{6,7},{7,6},{8,9},{9,8},{10,11... | collective-permute-start | bytes 1179656 | tf_op jit(solution)/shard_map/ppermute | solution.py:332
  7.4 5.2 %copy-start.4 = (bf16[2048,64]{0,1:T(8,128)(2,1)S(1)}, bf16[2048,64]{0,1:T(8,128)(2,1)}, u32[]{:S(2)}) copy-start(bf16[2048,64]{0,1:T(8,128)(2,1)} %param.17) | copy-start | bytes 786436
  7.4 5.2 %copy-start.5 = (bf16[2048,64]{0,1:T(8,128)(2,1)S(1)}, bf16[2048,64]{0,1:T(8,128)(2,1)}, u32[]{:S(2)}) copy-start(bf16[2048,64]{0,1:T(8,128)(2,1)} %param.21) | copy-start | bytes 786436
  11.0 23.3 %collective-permute-start.10 = (bf16[128,1536]{1,0:T(8,128)(2,1)S(1)}, bf16[128,1536]{1,0:T(8,128)(2,1)S(1)}, u32[]{:S(2)}, u32[]{:S(2)}) collective-permute-start(bf16[128,1536]{1,0:T(8,128)(2,1)S(1)} %get-tuple-element.32.refs_8_), channel_id=1, source_target_pairs={{0,2},{1,3},{2,0},{3,1},{4,6},{5,7},{6,4},{7,5},{8,10},{9,11},{10,... | collective-permute-start | bytes 1179656 | tf_op jit(solution)/shard_map/ppermute | solution.py:332
  16.2 28.7 %collective-permute-start.8 = (bf16[128,1664]{1,0:T(8,128)(2,1)S(1)}, bf16[128,1664]{1,0:T(8,128)(2,1)S(1)}, u32[]{:S(2)}, u32[]{:S(2)}) collective-permute-start(bf16[128,1664]{1,0:T(8,128)(2,1)S(1)} %get-tuple-element.34.refs_6_), channel_id=1, source_target_pairs={{0,1},{1,0},{2,3},{3,2},{4,5},{5,4},{6,7},{7,6},{8,9},{9,8},{10,11... | collective-permute-start | bytes 1277960 | tf_op jit(solution)/shard_map/ppermute | solution.py:332
  20.3 14.6 %collective-permute-start.6 = (bf16[128,1536]{1,0:T(8,128)(2,1)S(1)}, bf16[128,1536]{1,0:T(8,128)(2,1)S(1)}, u32[]{:S(2)}, u32[]{:S(2)}) collective-permute-start(bf16[128,1536]{1,0:T(8,128)(2,1)S(1)} %get-tuple-element.36.refs_6_), channel_id=1, source_target_pairs={{0,2},{1,3},{2,0},{3,1},{4,6},{5,7},{6,4},{7,5},{8,10},{9,11},{10,... | collective-permute-start | bytes 1179656 | tf_op jit(solution)/shard_map/ppermute | solution.py:332
  24.0 12.2 %collective-permute-start.4 = (bf16[128,1536]{1,0:T(8,128)(2,1)S(1)}, bf16[128,1536]{1,0:T(8,128)(2,1)S(1)}, u32[]{:S(2)}, u32[]{:S(2)}) collective-permute-start(bf16[128,1536]{1,0:T(8,128)(2,1)S(1)} %get-tuple-element.38.refs_6_), channel_id=1, source_target_pairs={{0,1},{1,0},{2,3},{3,2},{4,5},{5,4},{6,7},{7,6},{8,9},{9,8},{10,11... | collective-permute-start | bytes 1179656 | tf_op jit(solution)/shard_map/ppermute | solution.py:332
  32.7 12.1 %collective-permute-start.2 = (bf16[128,1536]{1,0:T(8,128)(2,1)S(1)}, bf16[128,1536]{1,0:T(8,128)(2,1)S(1)}, u32[]{:S(2)}, u32[]{:S(2)}) collective-permute-start(bf16[128,1536]{1,0:T(8,128)(2,1)S(1)} %get-tuple-element.40.refs_6_), channel_id=1, source_target_pairs={{0,2},{1,3},{2,0},{3,1},{4,6},{5,7},{6,4},{7,5},{8,10},{9,11},{10,... | collective-permute-start | bytes 1179656 | tf_op jit(solution)/shard_map/ppermute | solution.py:332
  34.2 16.9 %copy-start = (bf16[3584,64]{0,1:T(8,128)(2,1)S(1)}, bf16[3584,64]{0,1:T(8,128)(2,1)}, u32[]{:S(2)}) copy-start(bf16[3584,64]{0,1:T(8,128)(2,1)} %param.18) | copy-start | bytes 1376260
  34.2 16.9 %copy-start.1 = (bf16[3584,64]{0,1:T(8,128)(2,1)S(1)}, bf16[3584,64]{0,1:T(8,128)(2,1)}, u32[]{:S(2)}) copy-start(bf16[3584,64]{0,1:T(8,128)(2,1)} %param.19) | copy-start | bytes 1376260
  34.2 16.9 %copy-start.2 = (bf16[3584,64]{0,1:T(8,128)(2,1)S(1)}, bf16[3584,64]{0,1:T(8,128)(2,1)}, u32[]{:S(2)}) copy-start(bf16[3584,64]{0,1:T(8,128)(2,1)} %param.20) | copy-start | bytes 1376260
  34.3 12.7 %collective-permute-start = (bf16[128,1536]{1,0:T(8,128)(2,1)S(1)}, bf16[128,1536]{1,0:T(8,128)(2,1)S(1)}, u32[]{:S(2)}, u32[]{:S(2)}) collective-permute-start(bf16[128,1536]{1,0:T(8,128)(2,1)S(1)} %get-tuple-element.42), channel_id=1, source_target_pairs={{0,1},{1,0},{2,3},{3,2},{4,5},{5,4},{6,7},{7,6},{8,9},{9,8},{10,11... | collective-permute-start | bytes 1179656 | tf_op jit(solution)/shard_map/ppermute | solution.py:332
  35.0 14.0 %collective-permute-start.13 = (bf16[64,1536]{1,0:T(8,128)(2,1)S(1)}, bf16[64,1536]{1,0:T(8,128)(2,1)S(1)}, u32[]{:S(2)}, u32[]{:S(2)}) collective-permute-start(bf16[64,1536]{1,0:T(8,128)(2,1)S(1)} %add_convert_fusion.1), channel_id=1, source_target_pairs={{0,2},{1,3},{2,0},{3,1},{4,6},{5,7},{6,4},{7,5},{8,10},{9,11},{10,... | collective-permute-start | bytes 589832 | tf_op jit(solution)/shard_map/ppermute | solution.py:332
  36.2 14.5 %collective-permute-start.11 = (bf16[64,1536]{1,0:T(8,128)(2,1)S(1)}, bf16[64,1536]{1,0:T(8,128)(2,1)S(1)}, u32[]{:S(2)}, u32[]{:S(2)}) collective-permute-start(bf16[64,1536]{1,0:T(8,128)(2,1)S(1)} %add_convert_fusion.2), channel_id=1, source_target_pairs={{0,1},{1,0},{2,3},{3,2},{4,5},{5,4},{6,7},{7,6},{8,9},{9,8},{10,11... | collective-permute-start | bytes 589832 | tf_op jit(solution)/shard_map/ppermute | solution.py:332
  44.8 12.8 %collective-permute-start.7 = (bf16[64,1536]{1,0:T(8,128)(2,1)S(1)}, bf16[64,1536]{1,0:T(8,128)(2,1)S(1)}, u32[]{:S(2)}, u32[]{:S(2)}) collective-permute-start(bf16[64,1536]{1,0:T(8,128)(2,1)S(1)} %add_convert_fusion.3), channel_id=1, source_target_pairs={{0,1},{1,0},{2,3},{3,2},{4,5},{5,4},{6,7},{7,6},{8,9},{9,8},{10,11... | collective-permute-start | bytes 589832 | tf_op jit(solution)/shard_map/ppermute | solution.py:332
  44.9 12.9 %collective-permute-start.5 = (bf16[64,1536]{1,0:T(8,128)(2,1)S(1)}, bf16[64,1536]{1,0:T(8,128)(2,1)S(1)}, u32[]{:S(2)}, u32[]{:S(2)}) collective-permute-start(bf16[64,1536]{1,0:T(8,128)(2,1)S(1)} %add_convert_fusion.4), channel_id=1, source_target_pairs={{0,2},{1,3},{2,0},{3,1},{4,6},{5,7},{6,4},{7,5},{8,10},{9,11},{10,... | collective-permute-start | bytes 589832 | tf_op jit(solution)/shard_map/ppermute | solution.py:332
  47.0 11.1 %collective-permute-start.3 = (bf16[64,1536]{1,0:T(8,128)(2,1)S(1)}, bf16[64,1536]{1,0:T(8,128)(2,1)S(1)}, u32[]{:S(2)}, u32[]{:S(2)}) collective-permute-start(bf16[64,1536]{1,0:T(8,128)(2,1)S(1)} %add_convert_fusion.5), channel_id=1, source_target_pairs={{0,1},{1,0},{2,3},{3,2},{4,5},{5,4},{6,7},{7,6},{8,9},{9,8},{10,11... | collective-permute-start | bytes 589832 | tf_op jit(solution)/shard_map/ppermute | solution.py:332
  49.0 8.3 %collective-permute-start.9 = (bf16[64,1664]{1,0:T(8,128)(2,1)S(1)}, bf16[64,1664]{1,0:T(8,128)(2,1)S(1)}, u32[]{:S(2)}, u32[]{:S(2)}) collective-permute-start(bf16[64,1664]{1,0:T(8,128)(2,1)S(1)} %add_convert_fusion), channel_id=1, source_target_pairs={{0,2},{1,3},{2,0},{3,1},{4,6},{5,7},{6,4},{7,5},{8,10},{9,11},{10,... | collective-permute-start | bytes 638984 | tf_op jit(solution)/shard_map/ppermute | solution.py:332
  50.6 8.7 %collective-permute-start.1 = (bf16[64,1536]{1,0:T(8,128)(2,1)S(1)}, bf16[64,1536]{1,0:T(8,128)(2,1)S(1)}, u32[]{:S(2)}, u32[]{:S(2)}) collective-permute-start(bf16[64,1536]{1,0:T(8,128)(2,1)S(1)} %add_convert_fusion.6), channel_id=1, source_target_pairs={{0,2},{1,3},{2,0},{3,1},{4,6},{5,7},{6,4},{7,5},{8,10},{9,11},{10,... | collective-permute-start | bytes 589832 | tf_op jit(solution)/shard_map/ppermute | solution.py:332
  58.3 17.9 %copy-start.3 = (bf16[128,12288]{1,0:T(8,128)(2,1)S(1)}, bf16[128,12288]{1,0:T(8,128)(2,1)}, u32[]{:S(2)}) copy-start(bf16[128,12288]{1,0:T(8,128)(2,1)} %refs_4_.15) | copy-start | bytes 9437188
  58.4 17.9 %copy-start.6 = (s32[1,128]{1,0:T(1,128)S(1)}, s32[1,128]{1,0:T(1,128)}, u32[]{:S(2)}) copy-start(s32[1,128]{1,0:T(1,128)} %refs_5_.3) | copy-start | bytes 1540
  59.9 1.3 %collective-permute-start.14 = (bf16[64,192]{1,0:T(8,128)(2,1)S(1)}, bf16[64,192]{1,0:T(8,128)(2,1)S(1)}, u32[]{:S(2)}, u32[]{:S(2)}) collective-permute-start(bf16[64,192]{1,0:T(8,128)(2,1)S(1)} %project_3072.1), channel_id=1, source_target_pairs={{0,4},{4,0},{8,12},{12,8},{16,20},{20,16},{24,28},{28,24},{1,5},{5... | collective-permute-start | bytes 73736 | tf_op jit(solution)/shard_map/ppermute | solution.py:332
  61.2 5.8 %collective-permute-start.17 = (bf16[64,192]{1,0:T(8,128)(2,1)S(1)}, bf16[64,192]{1,0:T(8,128)(2,1)S(1)}, u32[]{:S(2)}, u32[]{:S(2)}) collective-permute-start(bf16[64,192]{1,0:T(8,128)(2,1)S(1)} %add_convert_fusion.8), channel_id=1, source_target_pairs={{0,24},{4,28},{8,16},{12,20},{16,8},{20,12},{24,0},{28,4},{1,25},{... | collective-permute-start | bytes 73736 | tf_op jit(solution)/shard_map/ppermute | solution.py:332
  64.9 4.8 %collective-permute-start.16 = (bf16[64,192]{1,0:T(8,128)(2,1)S(1)}, bf16[64,192]{1,0:T(8,128)(2,1)S(1)}, u32[]{:S(2)}, u32[]{:S(2)}) collective-permute-start(bf16[64,192]{1,0:T(8,128)(2,1)S(1)} %add_convert_fusion.8), channel_id=1, source_target_pairs={{0,16},{4,20},{8,24},{12,28},{16,0},{20,4},{24,8},{28,12},{1,17},{... | collective-permute-start | bytes 73736 | tf_op jit(solution)/shard_map/ppermute | solution.py:332
  64.9 4.8 %collective-permute-start.15 = (bf16[64,192]{1,0:T(8,128)(2,1)S(1)}, bf16[64,192]{1,0:T(8,128)(2,1)S(1)}, u32[]{:S(2)}, u32[]{:S(2)}) collective-permute-start(bf16[64,192]{1,0:T(8,128)(2,1)S(1)} %add_convert_fusion.8), channel_id=1, source_target_pairs={{0,8},{4,12},{8,0},{12,4},{16,24},{20,28},{24,16},{28,20},{1,9},{5... | collective-permute-start | bytes 73736 | tf_op jit(solution)/shard_map/ppermute | solution.py:332
  70.1 5.2 %collective-permute-start.20 = (bf16[1,12288]{1,0:T(2,128)(2,1)S(1)}, bf16[1,12288]{1,0:T(2,128)(2,1)S(1)}, u32[]{:S(2)}, u32[]{:S(2)}) collective-permute-start(bf16[1,12288]{1,0:T(2,128)(2,1)S(1)} %constant_dynamic-update-slice_fusion.refs_0_), channel_id=1, source_target_pairs={{0,3},{1,2},{2,1},{3,0},{4,7},{5,6},{6,5},{7,4},{8,11},{9,10},{10,... | collective-permute-start | bytes 73736 | tf_op jit(solution)/shard_map/ppermute | solution.py:332
  71.7 4.2 %collective-permute-start.19 = (bf16[1,12288]{1,0:T(2,128)(2,1)S(1)}, bf16[1,12288]{1,0:T(2,128)(2,1)S(1)}, u32[]{:S(2)}, u32[]{:S(2)}) collective-permute-start(bf16[1,12288]{1,0:T(2,128)(2,1)S(1)} %constant_dynamic-update-slice_fusion.refs_0_), channel_id=1, source_target_pairs={{0,2},{1,3},{2,0},{3,1},{4,6},{5,7},{6,4},{7,5},{8,10},{9,11},{10,... | collective-permute-start | bytes 73736 | tf_op jit(solution)/shard_map/ppermute | solution.py:332
  72.2 4.1 %collective-permute-start.18 = (bf16[1,12288]{1,0:T(2,128)(2,1)S(1)}, bf16[1,12288]{1,0:T(2,128)(2,1)S(1)}, u32[]{:S(2)}, u32[]{:S(2)}) collective-permute-start(bf16[1,12288]{1,0:T(2,128)(2,1)S(1)} %constant_dynamic-update-slice_fusion.refs_0_), channel_id=1, source_target_pairs={{0,1},{1,0},{2,3},{3,2},{4,5},{5,4},{6,7},{7,6},{8,9},{9,8},{10,11... | collective-permute-start | bytes 73736 | tf_op jit(solution)/shard_map/ppermute | solution.py:332

commit v3 on v2

--- a/solution.py
+++ b/solution.py
@@ -207,7 +207,7 @@
     p_gate, p_up, p_hidden = refs[:3]
     refs = refs[3:]
     before = refs[0]
-    out = refs[-1]
+    out = refs[1 + (sums[0] if sums else 0)]
     whole = sum(columns for _, columns in pieces)
 
     def total(refs, at, columns):
@@ -244,15 +244,24 @@
             a, b, TN, preferred_element_type=F32, precision=lax.Precision.HIGHEST
         )
 
-    out[:, : 2 * rank] = outer(both[:, :rank], part[:, : 2 * rank]).astype(BF16)
-    out[:, 2 * rank :] = outer(part[:, 2 * rank :], both[:, rank:]).astype(BF16)
+    first_two = outer(both[:, :rank], part[:, : 2 * rank])
+    products = (
+        first_two[:, :rank],
+        first_two[:, rank:],
+        outer(part[:, 2 * rank :], both[:, rank:]),
+    )
+    half = rank // 2
+    for number, (product, held) in enumerate(zip(products, refs[-3:])):
+        held[...] = product
+        pairs = [held[pl.ds(odd, half, stride=2), :] for odd in range(2)]
+        out[number * half : (number + 1) * half, :] = jnp.concatenate(pairs, axis=1).astype(BF16)
 
 
 def project(addends, projections, before, first, pieces, sums=(), at=0):
     rank = projections[0].shape[0]
     vmem = pl.BlockSpec(memory_space=pltpu.VMEM)
     shape = (
-        jax.ShapeDtypeStruct((rank, 3 * rank), BF16)
+        jax.ShapeDtypeStruct((3 * rank // 2, 2 * rank), BF16)
         if sums
         else jax.ShapeDtypeStruct(before.shape, F32)
     )
@@ -268,6 +277,7 @@
         out_shape=shape,
         in_specs=[vmem] * (len(addends) + 4 + len(sums)),
         out_specs=vmem,
+        scratch_shapes=[pltpu.VMEM((rank, rank), F32)] * (3 if sums else 0),
         compiler_params=pltpu.CompilerParams(vmem_limit_bytes=16 << 20),
         cost_estimate=pl.CostEstimate(
             flops=6 * SEQ_LEN * rank * sum(c for _, c in pieces),
@@ -281,14 +291,19 @@
 def score_kernel(count, e_ref, *refs):
     queries, (store, ids, out, rows) = refs[:count], refs[count:]
     for j in range(count):
-        rows[pl.ds(e_ref[0] ^ j, 1), :] = queries[j][...].astype(F32)
+        query = queries[j][...].astype(F32)
+        lanes = query.shape[1]
+        for p in range(query.shape[0]):
+            rows[j : j + 1, p * lanes : (p + 1) * lanes] = query[p : p + 1, :]
     lhs = rows[...].astype(BF16)
     natural = lax.dot_general(lhs, store[...], NT, preferred_element_type=F32)
     docs = store.shape[0]
     chosen = lax.broadcasted_iota(jnp.int32, (docs, docs), 0) == ids[...]
-    out[...] = jnp.dot(
+    scores = jnp.dot(
         natural, chosen.astype(F32), preferred_element_type=F32, precision=lax.Precision.HIGHEST
     )
+    for j in range(count):
+        out[pl.ds(e_ref[0] ^ j, 1), :] = scores[j : j + 1, :]
 
 
 def score(index, queries, store, ids):
@@ -442,10 +457,7 @@
     whole = functools.reduce(
         jnp.add, [pair.astype(F32)] + [flip(pair, "tensor", k).astype(F32) for k in range(2, tensor, 2)]
     ).astype(BF16)
-    query = jnp.concatenate(
-        [whole[:, m * rank : (m + 1) * rank].reshape(1, rank * rank) for m in range(3)], axis=1
-    )
-    queries = [query] + [flip(query, "example", k) for k in range(1, example)]
+    queries = [whole] + [flip(whole, "example", k) for k in range(1, example)]
     return score(index, queries, store, doc_ids)
 
 

time: 78.2 us -> 77.4 us (0.990)
  no operation moved by 1% of the time
where the time goes in v3:
time: 77.4 us; the launch traced here: 77.3 us
  Pallas kernels  29.1 us (38%)
  starting transfers between devices  24.4 us (32%)
  waiting for transfers between devices  23.1 us (30%)
    pallas_call x7, Pallas kernels, partials(): pl.pallas_call(functools.partial(partials_kernel, count, groups, opening,...  25.3 us
    ppermute x21, starting transfers between devices, flip(): return lax.ppermute(x, axis, [(i, i ^ k) for i in range(n)])  24.4 us
    ppermute x21, waiting for transfers between devices, flip(): return lax.ppermute(x, axis, [(i, i ^ k) for i in range(n)])  23.1 us
    pallas_call x7, Pallas kernels, project(): pl.pallas_call(functools.partial(project_kernel, len(addends), pieces, fi...  2.12 us
    pallas_call x1, Pallas kernels, score(): pl.pallas_call(functools.partial(score_kernel, count), out_shape=jax.Shap...  1.72 us
  transfers between devices with their start and end apart: 21, of which 12 were waited for; matrix products, arithmetic and copies ran while one was open for 0% of the time, Pallas kernels for 29%

profile of v3, /device:TPU:0, one launch (start us, length us, event | category | flops | bytes accessed | tf_op | source)
XLA Modules:
  0.0 77.3 jit_solution(15516921674391205883)
XLA Ops:
  0.0 4.4 %partials_0.1 = (bf16[128,1536]{1,0:T(8,128)(2,1)S(1)}, bf16[128,1536]{1,0:T(8,128)(2,1)S(1)}, bf16[256,2048]{1,0:T(8,128)(2,1)S(1)}, bf16[256,2048]{1,0:T(8,128)(2,1)S(1)}, bf16[2048,512]{1,0:T(8,128)(2,1)S(1)}) custom-call(s32[1]{0:T(128)} %bitcast.refs_0_.e_ref, bf16[256,2048]{1,0:T(8,128)(2,1)} %refs_1_.1, bf16[256,2048]{1,0:T(8,128)(2,1)} %refs_2_.7, ...), custom_call_target="tpu_custom_call" | custom-call | flops 1610612736 | bytes 7077888 | tf_op jit(solution)/shard_map/partials_0/pallas_call | solution.py:165
  4.4 3.0 %collective-permute-start.12 = (bf16[128,1536]{1,0:T(8,128)(2,1)S(1)}, bf16[128,1536]{1,0:T(8,128)(2,1)S(1)}, u32[]{:S(2)}, u32[]{:S(2)}) collective-permute-start(bf16[128,1536]{1,0:T(8,128)(2,1)S(1)} %get-tuple-element.30.refs_6_), channel_id=1, source_target_pairs={{0,1},{1,0},{2,3},{3,2},{4,5},{5,4},{6,7},{7,6},{8,9},{9,8},{10,11... | collective-permute-start | bytes 1179656 | tf_op jit(solution)/shard_map/ppermute | solution.py:347
  7.4 3.6 %partials_512.1 = (bf16[128,1536]{1,0:T(8,128)(2,1)S(1)}, bf16[128,1536]{1,0:T(8,128)(2,1)S(1)}, bf16[2048,512]{1,0:T(8,128)(2,1)S(1)}) custom-call(bf16[256,2048]{1,0:T(8,128)(2,1)S(1)} %get-tuple-element.27.refs_0_, bf16[256,2048]{1,0:T(8,128)(2,1)S(1)} %get-tuple-element.28.refs_1_, bf16[2048,3584]{1,0:T(8,128)(2,1)} %refs_2_.13, ...), custom_call_target="tpu_custom_call" | custom-call | flops 1610612736 | bytes 7077888 | tf_op jit(solution)/shard_map/partials_512/pallas_call | solution.py:165
  11.0 1.6 %collective-permute-start.10 = (bf16[128,1536]{1,0:T(8,128)(2,1)S(1)}, bf16[128,1536]{1,0:T(8,128)(2,1)S(1)}, u32[]{:S(2)}, u32[]{:S(2)}) collective-permute-start(bf16[128,1536]{1,0:T(8,128)(2,1)S(1)} %get-tuple-element.32.refs_8_), channel_id=1, source_target_pairs={{0,2},{1,3},{2,0},{3,1},{4,6},{5,7},{6,4},{7,5},{8,10},{9,11},{10,... | collective-permute-start | bytes 1179656 | tf_op jit(solution)/shard_map/ppermute | solution.py:347
  12.6 3.6 %partials_1024.1 = (bf16[128,1664]{1,0:T(8,128)(2,1)S(1)}, bf16[128,1664]{1,0:T(8,128)(2,1)S(1)}, bf16[2048,512]{1,0:T(8,128)(2,1)S(1)}) custom-call(bf16[256,2048]{1,0:T(8,128)(2,1)S(1)} %get-tuple-element.27.refs_0_, bf16[256,2048]{1,0:T(8,128)(2,1)S(1)} %get-tuple-element.28.refs_1_, bf16[2048,3584]{1,0:T(8,128)(2,1)} %refs_2_.13, ...), custom_call_target="tpu_custom_call" | custom-call | flops 1744830464 | bytes 7143424 | tf_op jit(solution)/shard_map/partials_1024/pallas_call | solution.py:165
  16.2 0.6 collective-permute-start.8
  16.8 3.5 %partials_1536.1 = (bf16[128,1536]{1,0:T(8,128)(2,1)S(1)}, bf16[128,1536]{1,0:T(8,128)(2,1)S(1)}, bf16[2048,512]{1,0:T(8,128)(2,1)S(1)}) custom-call(bf16[256,2048]{1,0:T(8,128)(2,1)S(1)} %get-tuple-element.27.refs_0_, bf16[256,2048]{1,0:T(8,128)(2,1)S(1)} %get-tuple-element.28.refs_1_, bf16[2048,3584]{1,0:T(8,128)(2,1)} %refs_2_.13, ...), custom_call_target="tpu_custom_call" | custom-call | flops 1610612736 | bytes 7077888 | tf_op jit(solution)/shard_map/partials_1536/pallas_call | solution.py:165
  20.3 0.1 collective-permute-start.6
  20.4 3.5 %partials_2048.1 = (bf16[128,1536]{1,0:T(8,128)(2,1)S(1)}, bf16[128,1536]{1,0:T(8,128)(2,1)S(1)}, bf16[2048,512]{1,0:T(8,128)(2,1)S(1)}) custom-call(bf16[256,2048]{1,0:T(8,128)(2,1)S(1)} %get-tuple-element.27.refs_0_, bf16[256,2048]{1,0:T(8,128)(2,1)S(1)} %get-tuple-element.28.refs_1_, bf16[2048,3584]{1,0:T(8,128)(2,1)} %refs_2_.13, ...), custom_call_target="tpu_custom_call" | custom-call | flops 1610612736 | bytes 7077888 | tf_op jit(solution)/shard_map/partials_2048/pallas_call | solution.py:165
  24.0 2.0 %collective-permute-start.4 = (bf16[128,1536]{1,0:T(8,128)(2,1)S(1)}, bf16[128,1536]{1,0:T(8,128)(2,1)S(1)}, u32[]{:S(2)}, u32[]{:S(2)}) collective-permute-start(bf16[128,1536]{1,0:T(8,128)(2,1)S(1)} %get-tuple-element.38.refs_6_), channel_id=1, source_target_pairs={{0,1},{1,0},{2,3},{3,2},{4,5},{5,4},{6,7},{7,6},{8,9},{9,8},{10,11... | collective-permute-start | bytes 1179656 | tf_op jit(solution)/shard_map/ppermute | solution.py:347
  26.0 3.5 %partials_2560.1 = (bf16[128,1536]{1,0:T(8,128)(2,1)S(1)}, bf16[128,1536]{1,0:T(8,128)(2,1)S(1)}, bf16[2048,512]{1,0:T(8,128)(2,1)S(1)}) custom-call(bf16[256,2048]{1,0:T(8,128)(2,1)S(1)} %get-tuple-element.27.refs_0_, bf16[256,2048]{1,0:T(8,128)(2,1)S(1)} %get-tuple-element.28.refs_1_, bf16[2048,3584]{1,0:T(8,128)(2,1)} %refs_2_.13, ...), custom_call_target="tpu_custom_call" | custom-call | flops 1610612736 | bytes 7077888 | tf_op jit(solution)/shard_map/partials_2560/pallas_call | solution.py:165
  29.6 3.1 %partials_3072.1 = (bf16[128,1536]{1,0:T(8,128)(2,1)S(1)}, bf16[128,1536]{1,0:T(8,128)(2,1)S(1)}) custom-call(bf16[256,2048]{1,0:T(8,128)(2,1)S(1)} %get-tuple-element.27.refs_0_, bf16[256,2048]{1,0:T(8,128)(2,1)S(1)} %get-tuple-element.28.refs_1_, bf16[2048,3584]{1,0:T(8,128)(2,1)} %refs_2_.13, bf16[2048,3584]{1,0:T(8,128)(2,1)} %refs_3_.13, ...), custom_call_target="tpu_custom_call" | custom-call | flops 1610612736 | bytes 7077888 | tf_op jit(solution)/shard_map/partials_3072/pallas_call | solution.py:165
  32.7 1.6 %collective-permute-start.2 = (bf16[128,1536]{1,0:T(8,128)(2,1)S(1)}, bf16[128,1536]{1,0:T(8,128)(2,1)S(1)}, u32[]{:S(2)}, u32[]{:S(2)}) collective-permute-start(bf16[128,1536]{1,0:T(8,128)(2,1)S(1)} %get-tuple-element.40.refs_6_), channel_id=1, source_target_pairs={{0,2},{1,3},{2,0},{3,1},{4,6},{5,7},{6,4},{7,5},{8,10},{9,11},{10,... | collective-permute-start | bytes 1179656 | tf_op jit(solution)/shard_map/ppermute | solution.py:347
  34.3 0.6 collective-permute-start
  35.0 0.1 collective-permute-start.13
  35.1 1.0 %collective-permute-done.4.refs_1_ = bf16[128,1536]{1,0:T(8,128)(2,1)S(1)} collective-permute-done((bf16[128,1536]{1,0:T(8,128)(2,1)S(1)}, bf16[128,1536]{1,0:T(8,128)(2,1)S(1)}, u32[]{:S(2)}, u32[]{:S(2)}) %collective-permute-start.4) | collective-permute-done | bytes 393248 | tf_op jit(solution)/shard_map/ppermute | solution.py:347
  36.2 1.0 %collective-permute-start.11 = (bf16[64,1536]{1,0:T(8,128)(2,1)S(1)}, bf16[64,1536]{1,0:T(8,128)(2,1)S(1)}, u32[]{:S(2)}, u32[]{:S(2)}) collective-permute-start(bf16[64,1536]{1,0:T(8,128)(2,1)S(1)} %add_convert_fusion.2), channel_id=1, source_target_pairs={{0,1},{1,0},{2,3},{3,2},{4,5},{5,4},{6,7},{7,6},{8,9},{9,8},{10,11... | collective-permute-start | bytes 589832 | tf_op jit(solution)/shard_map/ppermute | solution.py:347
  37.2 7.6 %collective-permute-done.2.refs_1_ = bf16[128,1536]{1,0:T(8,128)(2,1)S(1)} collective-permute-done((bf16[128,1536]{1,0:T(8,128)(2,1)S(1)}, bf16[128,1536]{1,0:T(8,128)(2,1)S(1)}, u32[]{:S(2)}, u32[]{:S(2)}) %collective-permute-start.2) | collective-permute-done | bytes 393248 | tf_op jit(solution)/shard_map/ppermute | solution.py:347
  44.8 0.1 collective-permute-start.7
  44.9 2.1 %collective-permute-start.5 = (bf16[64,1536]{1,0:T(8,128)(2,1)S(1)}, bf16[64,1536]{1,0:T(8,128)(2,1)S(1)}, u32[]{:S(2)}, u32[]{:S(2)}) collective-permute-start(bf16[64,1536]{1,0:T(8,128)(2,1)S(1)} %add_convert_fusion.4), channel_id=1, source_target_pairs={{0,2},{1,3},{2,0},{3,1},{4,6},{5,7},{6,4},{7,5},{8,10},{9,11},{10,... | collective-permute-start | bytes 589832 | tf_op jit(solution)/shard_map/ppermute | solution.py:347
  47.0 0.1 add_convert_fusion
  47.0 1.6 %collective-permute-start.3 = (bf16[64,1536]{1,0:T(8,128)(2,1)S(1)}, bf16[64,1536]{1,0:T(8,128)(2,1)S(1)}, u32[]{:S(2)}, u32[]{:S(2)}) collective-permute-start(bf16[64,1536]{1,0:T(8,128)(2,1)S(1)} %add_convert_fusion.5), channel_id=1, source_target_pairs={{0,1},{1,0},{2,3},{3,2},{4,5},{5,4},{6,7},{7,6},{8,9},{9,8},{10,11... | collective-permute-start | bytes 589832 | tf_op jit(solution)/shard_map/ppermute | solution.py:347
  48.6 0.4 collective-permute-done.13.refs_2_
  49.0 1.5 %collective-permute-start.9 = (bf16[64,1664]{1,0:T(8,128)(2,1)S(1)}, bf16[64,1664]{1,0:T(8,128)(2,1)S(1)}, u32[]{:S(2)}, u32[]{:S(2)}) collective-permute-start(bf16[64,1664]{1,0:T(8,128)(2,1)S(1)} %add_convert_fusion), channel_id=1, source_target_pairs={{0,2},{1,3},{2,0},{3,1},{4,6},{5,7},{6,4},{7,5},{8,10},{9,11},{10,... | collective-permute-start | bytes 638984 | tf_op jit(solution)/shard_map/ppermute | solution.py:347
  50.6 0.1 collective-permute-done.11.refs_2_
  50.6 0.5 collective-permute-start.1
  51.2 0.3 project_0.1.refs_6_
  51.4 0.3 project_512.1.refs_6_
  51.7 5.6 %collective-permute-done.9.refs_2_.refs_9_ = bf16[64,1664]{1,0:T(8,128)(2,1)S(1)} collective-permute-done((bf16[64,1664]{1,0:T(8,128)(2,1)S(1)}, bf16[64,1664]{1,0:T(8,128)(2,1)S(1)}, u32[]{:S(2)}, u32[]{:S(2)}) %collective-permute-start.9) | collective-permute-done | bytes 213024 | tf_op jit(solution)/shard_map/ppermute | solution.py:347
  57.3 0.3 project_1024.1.refs_6_
  57.5 0.3 project_1536.1.refs_6_
  57.8 0.3 project_2048.1.refs_6_
  58.1 0.3 project_2560.1.refs_6_
  58.4 1.0 %collective-permute-done.1.refs_2_ = bf16[64,1536]{1,0:T(8,128)(2,1)S(1)} collective-permute-done((bf16[64,1536]{1,0:T(8,128)(2,1)S(1)}, bf16[64,1536]{1,0:T(8,128)(2,1)S(1)}, u32[]{:S(2)}, u32[]{:S(2)}) %collective-permute-start.1) | collective-permute-done | bytes 196640 | tf_op jit(solution)/shard_map/ppermute | solution.py:347
  59.4 0.6 project_3072.1
  60.0 0.1 collective-permute-start.14
  60.0 1.2 %collective-permute-done.14 = bf16[96,128]{1,0:T(8,128)(2,1)S(1)} collective-permute-done((bf16[96,128]{1,0:T(8,128)(2,1)S(1)}, bf16[96,128]{1,0:T(8,128)(2,1)S(1)}, u32[]{:S(2)}, u32[]{:S(2)}) %collective-permute-start.14) | collective-permute-done | bytes 24608 | tf_op jit(solution)/shard_map/ppermute | solution.py:347
  61.2 3.7 %collective-permute-start.17 = (bf16[96,128]{1,0:T(8,128)(2,1)S(1)}, bf16[96,128]{1,0:T(8,128)(2,1)S(1)}, u32[]{:S(2)}, u32[]{:S(2)}) collective-permute-start(bf16[96,128]{1,0:T(8,128)(2,1)S(1)} %add_convert_fusion.8), channel_id=1, source_target_pairs={{0,24},{4,28},{8,16},{12,20},{16,8},{20,12},{24,0},{28,4},{1,25},{... | collective-permute-start | bytes 73736 | tf_op jit(solution)/shard_map/ppermute | solution.py:347
  64.9 0.8 %collective-permute-start.15 = (bf16[96,128]{1,0:T(8,128)(2,1)S(1)}, bf16[96,128]{1,0:T(8,128)(2,1)S(1)}, u32[]{:S(2)}, u32[]{:S(2)}) collective-permute-start(bf16[96,128]{1,0:T(8,128)(2,1)S(1)} %add_convert_fusion.8), channel_id=1, source_target_pairs={{0,8},{4,12},{8,0},{12,4},{16,24},{20,28},{24,16},{28,20},{1,9},{5... | collective-permute-start | bytes 73736 | tf_op jit(solution)/shard_map/ppermute | solution.py:347
  65.7 1.2 %collective-permute-done.17 = bf16[96,128]{1,0:T(8,128)(2,1)S(1)} collective-permute-done((bf16[96,128]{1,0:T(8,128)(2,1)S(1)}, bf16[96,128]{1,0:T(8,128)(2,1)S(1)}, u32[]{:S(2)}, u32[]{:S(2)}) %collective-permute-start.17) | collective-permute-done | bytes 24608 | tf_op jit(solution)/shard_map/ppermute | solution.py:347
  66.9 2.7 %collective-permute-done.16 = bf16[96,128]{1,0:T(8,128)(2,1)S(1)} collective-permute-done((bf16[96,128]{1,0:T(8,128)(2,1)S(1)}, bf16[96,128]{1,0:T(8,128)(2,1)S(1)}, u32[]{:S(2)}, u32[]{:S(2)}) %collective-permute-start.16) | collective-permute-done | bytes 24608 | tf_op jit(solution)/shard_map/ppermute | solution.py:347
  69.7 1.5 %collective-permute-start.20 = (bf16[96,128]{1,0:T(8,128)(2,1)S(1)}, bf16[96,128]{1,0:T(8,128)(2,1)S(1)}, u32[]{:S(2)}, u32[]{:S(2)}) collective-permute-start(bf16[96,128]{1,0:T(8,128)(2,1)S(1)} %add_convert_fusion.7.refs_0_), channel_id=1, source_target_pairs={{0,3},{1,2},{2,1},{3,0},{4,7},{5,6},{6,5},{7,4},{8,11},{9,10},{10,... | collective-permute-start | bytes 73736 | tf_op jit(solution)/shard_map/ppermute | solution.py:347
  71.2 0.5 collective-permute-start.19
  71.7 1.5 %collective-permute-start.18 = (bf16[96,128]{1,0:T(8,128)(2,1)S(1)}, bf16[96,128]{1,0:T(8,128)(2,1)S(1)}, u32[]{:S(2)}, u32[]{:S(2)}) collective-permute-start(bf16[96,128]{1,0:T(8,128)(2,1)S(1)} %add_convert_fusion.7.refs_0_), channel_id=1, source_target_pairs={{0,1},{1,0},{2,3},{3,2},{4,5},{5,4},{6,7},{7,6},{8,9},{9,8},{10,11... | collective-permute-start | bytes 73736 | tf_op jit(solution)/shard_map/ppermute | solution.py:347
  73.2 1.2 %collective-permute-done.20.refs_3_ = bf16[96,128]{1,0:T(8,128)(2,1)S(1)} collective-permute-done((bf16[96,128]{1,0:T(8,128)(2,1)S(1)}, bf16[96,128]{1,0:T(8,128)(2,1)S(1)}, u32[]{:S(2)}, u32[]{:S(2)}) %collective-permute-start.20) | collective-permute-done | bytes 24608 | tf_op jit(solution)/shard_map/ppermute | solution.py:347
  74.5 0.6 collective-permute-done.19.refs_2_
  75.0 0.5 collective-permute-done.18.refs_1_
  75.6 1.7 %score.1 = f32[4,128]{1,0:T(4,128)} custom-call(s32[1]{0:T(128)} %bitcast.refs_0_.e_ref, bf16[96,128]{1,0:T(8,128)(2,1)S(1)} %add_convert_fusion.7.refs_0_, bf16[96,128]{1,0:T(8,128)(2,1)S(1)} %collective-permute-done.18.refs_1_, bf16[96,128]{1,0:T(8,128)(2,1)S(1)} %collective-permute-done.19.refs_2_, bf16[96,128]{1,0:T(8,128)(2,1)S(1)} %collective-permute-done.20.refs_3_, ...), custom_call_target="tpu_custom_call" | custom-call | tf_op jit(solution)/shard_map/score/pallas_call | solution.py:313
  (33 shorter events, 0.4 us)
Async XLA Ops:
  4.4 28.2 %collective-permute-start.12 = (bf16[128,1536]{1,0:T(8,128)(2,1)S(1)}, bf16[128,1536]{1,0:T(8,128)(2,1)S(1)}, u32[]{:S(2)}, u32[]{:S(2)}) collective-permute-start(bf16[128,1536]{1,0:T(8,128)(2,1)S(1)} %get-tuple-element.30.refs_6_), channel_id=1, source_target_pairs={{0,1},{1,0},{2,3},{3,2},{4,5},{5,4},{6,7},{7,6},{8,9},{9,8},{10,11... | collective-permute-start | bytes 1179656 | tf_op jit(solution)/shard_map/ppermute | solution.py:347
  7.4 5.2 %copy-start.4 = (bf16[2048,64]{0,1:T(8,128)(2,1)S(1)}, bf16[2048,64]{0,1:T(8,128)(2,1)}, u32[]{:S(2)}) copy-start(bf16[2048,64]{0,1:T(8,128)(2,1)} %param.17) | copy-start | bytes 786436
  7.4 5.2 %copy-start.5 = (bf16[2048,64]{0,1:T(8,128)(2,1)S(1)}, bf16[2048,64]{0,1:T(8,128)(2,1)}, u32[]{:S(2)}) copy-start(bf16[2048,64]{0,1:T(8,128)(2,1)} %param.21) | copy-start | bytes 786436
  11.0 23.3 %collective-permute-start.10 = (bf16[128,1536]{1,0:T(8,128)(2,1)S(1)}, bf16[128,1536]{1,0:T(8,128)(2,1)S(1)}, u32[]{:S(2)}, u32[]{:S(2)}) collective-permute-start(bf16[128,1536]{1,0:T(8,128)(2,1)S(1)} %get-tuple-element.32.refs_8_), channel_id=1, source_target_pairs={{0,2},{1,3},{2,0},{3,1},{4,6},{5,7},{6,4},{7,5},{8,10},{9,11},{10,... | collective-permute-start | bytes 1179656 | tf_op jit(solution)/shard_map/ppermute | solution.py:347
  16.2 28.7 %collective-permute-start.8 = (bf16[128,1664]{1,0:T(8,128)(2,1)S(1)}, bf16[128,1664]{1,0:T(8,128)(2,1)S(1)}, u32[]{:S(2)}, u32[]{:S(2)}) collective-permute-start(bf16[128,1664]{1,0:T(8,128)(2,1)S(1)} %get-tuple-element.34.refs_6_), channel_id=1, source_target_pairs={{0,1},{1,0},{2,3},{3,2},{4,5},{5,4},{6,7},{7,6},{8,9},{9,8},{10,11... | collective-permute-start | bytes 1277960 | tf_op jit(solution)/shard_map/ppermute | solution.py:347
  20.3 14.6 %collective-permute-start.6 = (bf16[128,1536]{1,0:T(8,128)(2,1)S(1)}, bf16[128,1536]{1,0:T(8,128)(2,1)S(1)}, u32[]{:S(2)}, u32[]{:S(2)}) collective-permute-start(bf16[128,1536]{1,0:T(8,128)(2,1)S(1)} %get-tuple-element.36.refs_6_), channel_id=1, source_target_pairs={{0,2},{1,3},{2,0},{3,1},{4,6},{5,7},{6,4},{7,5},{8,10},{9,11},{10,... | collective-permute-start | bytes 1179656 | tf_op jit(solution)/shard_map/ppermute | solution.py:347
  24.0 12.2 %collective-permute-start.4 = (bf16[128,1536]{1,0:T(8,128)(2,1)S(1)}, bf16[128,1536]{1,0:T(8,128)(2,1)S(1)}, u32[]{:S(2)}, u32[]{:S(2)}) collective-permute-start(bf16[128,1536]{1,0:T(8,128)(2,1)S(1)} %get-tuple-element.38.refs_6_), channel_id=1, source_target_pairs={{0,1},{1,0},{2,3},{3,2},{4,5},{5,4},{6,7},{7,6},{8,9},{9,8},{10,11... | collective-permute-start | bytes 1179656 | tf_op jit(solution)/shard_map/ppermute | solution.py:347
  32.7 12.1 %collective-permute-start.2 = (bf16[128,1536]{1,0:T(8,128)(2,1)S(1)}, bf16[128,1536]{1,0:T(8,128)(2,1)S(1)}, u32[]{:S(2)}, u32[]{:S(2)}) collective-permute-start(bf16[128,1536]{1,0:T(8,128)(2,1)S(1)} %get-tuple-element.40.refs_6_), channel_id=1, source_target_pairs={{0,2},{1,3},{2,0},{3,1},{4,6},{5,7},{6,4},{7,5},{8,10},{9,11},{10,... | collective-permute-start | bytes 1179656 | tf_op jit(solution)/shard_map/ppermute | solution.py:347
  34.2 16.9 %copy-start = (bf16[3584,64]{0,1:T(8,128)(2,1)S(1)}, bf16[3584,64]{0,1:T(8,128)(2,1)}, u32[]{:S(2)}) copy-start(bf16[3584,64]{0,1:T(8,128)(2,1)} %param.18) | copy-start | bytes 1376260
  34.2 16.9 %copy-start.1 = (bf16[3584,64]{0,1:T(8,128)(2,1)S(1)}, bf16[3584,64]{0,1:T(8,128)(2,1)}, u32[]{:S(2)}) copy-start(bf16[3584,64]{0,1:T(8,128)(2,1)} %param.19) | copy-start | bytes 1376260
  34.2 16.9 %copy-start.2 = (bf16[3584,64]{0,1:T(8,128)(2,1)S(1)}, bf16[3584,64]{0,1:T(8,128)(2,1)}, u32[]{:S(2)}) copy-start(bf16[3584,64]{0,1:T(8,128)(2,1)} %param.20) | copy-start | bytes 1376260
  34.3 12.7 %collective-permute-start = (bf16[128,1536]{1,0:T(8,128)(2,1)S(1)}, bf16[128,1536]{1,0:T(8,128)(2,1)S(1)}, u32[]{:S(2)}, u32[]{:S(2)}) collective-permute-start(bf16[128,1536]{1,0:T(8,128)(2,1)S(1)} %get-tuple-element.42), channel_id=1, source_target_pairs={{0,1},{1,0},{2,3},{3,2},{4,5},{5,4},{6,7},{7,6},{8,9},{9,8},{10,11... | collective-permute-start | bytes 1179656 | tf_op jit(solution)/shard_map/ppermute | solution.py:347
  35.0 14.0 %collective-permute-start.13 = (bf16[64,1536]{1,0:T(8,128)(2,1)S(1)}, bf16[64,1536]{1,0:T(8,128)(2,1)S(1)}, u32[]{:S(2)}, u32[]{:S(2)}) collective-permute-start(bf16[64,1536]{1,0:T(8,128)(2,1)S(1)} %add_convert_fusion.1), channel_id=1, source_target_pairs={{0,2},{1,3},{2,0},{3,1},{4,6},{5,7},{6,4},{7,5},{8,10},{9,11},{10,... | collective-permute-start | bytes 589832 | tf_op jit(solution)/shard_map/ppermute | solution.py:347
  36.2 14.5 %collective-permute-start.11 = (bf16[64,1536]{1,0:T(8,128)(2,1)S(1)}, bf16[64,1536]{1,0:T(8,128)(2,1)S(1)}, u32[]{:S(2)}, u32[]{:S(2)}) collective-permute-start(bf16[64,1536]{1,0:T(8,128)(2,1)S(1)} %add_convert_fusion.2), channel_id=1, source_target_pairs={{0,1},{1,0},{2,3},{3,2},{4,5},{5,4},{6,7},{7,6},{8,9},{9,8},{10,11... | collective-permute-start | bytes 589832 | tf_op jit(solution)/shard_map/ppermute | solution.py:347
  44.8 12.8 %collective-permute-start.7 = (bf16[64,1536]{1,0:T(8,128)(2,1)S(1)}, bf16[64,1536]{1,0:T(8,128)(2,1)S(1)}, u32[]{:S(2)}, u32[]{:S(2)}) collective-permute-start(bf16[64,1536]{1,0:T(8,128)(2,1)S(1)} %add_convert_fusion.3), channel_id=1, source_target_pairs={{0,1},{1,0},{2,3},{3,2},{4,5},{5,4},{6,7},{7,6},{8,9},{9,8},{10,11... | collective-permute-start | bytes 589832 | tf_op jit(solution)/shard_map/ppermute | solution.py:347
  44.9 12.9 %collective-permute-start.5 = (bf16[64,1536]{1,0:T(8,128)(2,1)S(1)}, bf16[64,1536]{1,0:T(8,128)(2,1)S(1)}, u32[]{:S(2)}, u32[]{:S(2)}) collective-permute-start(bf16[64,1536]{1,0:T(8,128)(2,1)S(1)} %add_convert_fusion.4), channel_id=1, source_target_pairs={{0,2},{1,3},{2,0},{3,1},{4,6},{5,7},{6,4},{7,5},{8,10},{9,11},{10,... | collective-permute-start | bytes 589832 | tf_op jit(solution)/shard_map/ppermute | solution.py:347
  47.0 11.1 %collective-permute-start.3 = (bf16[64,1536]{1,0:T(8,128)(2,1)S(1)}, bf16[64,1536]{1,0:T(8,128)(2,1)S(1)}, u32[]{:S(2)}, u32[]{:S(2)}) collective-permute-start(bf16[64,1536]{1,0:T(8,128)(2,1)S(1)} %add_convert_fusion.5), channel_id=1, source_target_pairs={{0,1},{1,0},{2,3},{3,2},{4,5},{5,4},{6,7},{7,6},{8,9},{9,8},{10,11... | collective-permute-start | bytes 589832 | tf_op jit(solution)/shard_map/ppermute | solution.py:347
  49.0 8.3 %collective-permute-start.9 = (bf16[64,1664]{1,0:T(8,128)(2,1)S(1)}, bf16[64,1664]{1,0:T(8,128)(2,1)S(1)}, u32[]{:S(2)}, u32[]{:S(2)}) collective-permute-start(bf16[64,1664]{1,0:T(8,128)(2,1)S(1)} %add_convert_fusion), channel_id=1, source_target_pairs={{0,2},{1,3},{2,0},{3,1},{4,6},{5,7},{6,4},{7,5},{8,10},{9,11},{10,... | collective-permute-start | bytes 638984 | tf_op jit(solution)/shard_map/ppermute | solution.py:347
  50.6 8.7 %collective-permute-start.1 = (bf16[64,1536]{1,0:T(8,128)(2,1)S(1)}, bf16[64,1536]{1,0:T(8,128)(2,1)S(1)}, u32[]{:S(2)}, u32[]{:S(2)}) collective-permute-start(bf16[64,1536]{1,0:T(8,128)(2,1)S(1)} %add_convert_fusion.6), channel_id=1, source_target_pairs={{0,2},{1,3},{2,0},{3,1},{4,6},{5,7},{6,4},{7,5},{8,10},{9,11},{10,... | collective-permute-start | bytes 589832 | tf_op jit(solution)/shard_map/ppermute | solution.py:347
  58.3 17.2 %copy-start.3 = (bf16[128,12288]{1,0:T(8,128)(2,1)S(1)}, bf16[128,12288]{1,0:T(8,128)(2,1)}, u32[]{:S(2)}) copy-start(bf16[128,12288]{1,0:T(8,128)(2,1)} %refs_4_.15) | copy-start | bytes 9437188
  58.4 17.2 %copy-start.6 = (s32[1,128]{1,0:T(1,128)S(1)}, s32[1,128]{1,0:T(1,128)}, u32[]{:S(2)}) copy-start(s32[1,128]{1,0:T(1,128)} %refs_5_.3) | copy-start | bytes 1540
  60.0 1.3 %collective-permute-start.14 = (bf16[96,128]{1,0:T(8,128)(2,1)S(1)}, bf16[96,128]{1,0:T(8,128)(2,1)S(1)}, u32[]{:S(2)}, u32[]{:S(2)}) collective-permute-start(bf16[96,128]{1,0:T(8,128)(2,1)S(1)} %project_3072.1), channel_id=1, source_target_pairs={{0,4},{4,0},{8,12},{12,8},{16,20},{20,16},{24,28},{28,24},{1,5},{5... | collective-permute-start | bytes 73736 | tf_op jit(solution)/shard_map/ppermute | solution.py:347
  61.2 5.7 %collective-permute-start.17 = (bf16[96,128]{1,0:T(8,128)(2,1)S(1)}, bf16[96,128]{1,0:T(8,128)(2,1)S(1)}, u32[]{:S(2)}, u32[]{:S(2)}) collective-permute-start(bf16[96,128]{1,0:T(8,128)(2,1)S(1)} %add_convert_fusion.8), channel_id=1, source_target_pairs={{0,24},{4,28},{8,16},{12,20},{16,8},{20,12},{24,0},{28,4},{1,25},{... | collective-permute-start | bytes 73736 | tf_op jit(solution)/shard_map/ppermute | solution.py:347
  64.9 4.7 %collective-permute-start.16 = (bf16[96,128]{1,0:T(8,128)(2,1)S(1)}, bf16[96,128]{1,0:T(8,128)(2,1)S(1)}, u32[]{:S(2)}, u32[]{:S(2)}) collective-permute-start(bf16[96,128]{1,0:T(8,128)(2,1)S(1)} %add_convert_fusion.8), channel_id=1, source_target_pairs={{0,16},{4,20},{8,24},{12,28},{16,0},{20,4},{24,8},{28,12},{1,17},{... | collective-permute-start | bytes 73736 | tf_op jit(solution)/shard_map/ppermute | solution.py:347
  64.9 4.7 %collective-permute-start.15 = (bf16[96,128]{1,0:T(8,128)(2,1)S(1)}, bf16[96,128]{1,0:T(8,128)(2,1)S(1)}, u32[]{:S(2)}, u32[]{:S(2)}) collective-permute-start(bf16[96,128]{1,0:T(8,128)(2,1)S(1)} %add_convert_fusion.8), channel_id=1, source_target_pairs={{0,8},{4,12},{8,0},{12,4},{16,24},{20,28},{24,16},{28,20},{1,9},{5... | collective-permute-start | bytes 73736 | tf_op jit(solution)/shard_map/ppermute | solution.py:347
  69.7 4.8 %collective-permute-start.20 = (bf16[96,128]{1,0:T(8,128)(2,1)S(1)}, bf16[96,128]{1,0:T(8,128)(2,1)S(1)}, u32[]{:S(2)}, u32[]{:S(2)}) collective-permute-start(bf16[96,128]{1,0:T(8,128)(2,1)S(1)} %add_convert_fusion.7.refs_0_), channel_id=1, source_target_pairs={{0,3},{1,2},{2,1},{3,0},{4,7},{5,6},{6,5},{7,4},{8,11},{9,10},{10,... | collective-permute-start | bytes 73736 | tf_op jit(solution)/shard_map/ppermute | solution.py:347
  71.2 3.8 %collective-permute-start.19 = (bf16[96,128]{1,0:T(8,128)(2,1)S(1)}, bf16[96,128]{1,0:T(8,128)(2,1)S(1)}, u32[]{:S(2)}, u32[]{:S(2)}) collective-permute-start(bf16[96,128]{1,0:T(8,128)(2,1)S(1)} %add_convert_fusion.7.refs_0_), channel_id=1, source_target_pairs={{0,2},{1,3},{2,0},{3,1},{4,6},{5,7},{6,4},{7,5},{8,10},{9,11},{10,... | collective-permute-start | bytes 73736 | tf_op jit(solution)/shard_map/ppermute | solution.py:347
  71.7 3.8 %collective-permute-start.18 = (bf16[96,128]{1,0:T(8,128)(2,1)S(1)}, bf16[96,128]{1,0:T(8,128)(2,1)S(1)}, u32[]{:S(2)}, u32[]{:S(2)}) collective-permute-start(bf16[96,128]{1,0:T(8,128)(2,1)S(1)} %add_convert_fusion.7.refs_0_), channel_id=1, source_target_pairs={{0,1},{1,0},{2,3},{3,2},{4,5},{5,4},{6,7},{7,6},{8,9},{9,8},{10,11... | collective-permute-start | bytes 73736 | tf_op jit(solution)/shard_map/ppermute | solution.py:347

commit v4 on v3

--- a/solution.py
+++ b/solution.py
@@ -386,7 +386,7 @@
         start = sum(len(c) for c in calls)
         calls.append(list(range(start, start + len(call))))
     widths = [sum(sizes[n][0] for n in call) for call in calls]
-    holder = calls[min(2, len(calls) - 1)][0]
+    holder = calls[min(4, len(calls) - 1)][0]
     acts_rows, grads_rows = acts, out_grad
     begun, done = [], []
     part = jnp.zeros((SEQ_LEN, 3 * rank), F32)

time: 77.4 us -> 77.4 us (level)
  starting transfers between devices: 24.4 us -> 25.4 us
  waiting for transfers between devices: 23.1 us -> 22.1 us
    ppermute x21, starting transfers between devices: 24.4 us -> 25.4 us  [flip(): return lax.ppermute(x, axis, [(i, i ^ k) for i in range(n)])]
    ppermute x21, waiting for transfers between devices: 23.1 us -> 22.1 us  [flip(): return lax.ppermute(x, axis, [(i, i ^ k) for i in range(n)])]
  transfers between devices with their start and end apart: 21 -> 21, of which waited for: 12 -> 13; matrix products, arithmetic and copies ran while one was open for 0% -> 0% of each run, Pallas kernels for 29% -> 29%
where the time goes in v4:
time: 77.4 us; the launch traced here: 77.3 us
  Pallas kernels  29.1 us (38%)
  starting transfers between devices  25.4 us (33%)
  waiting for transfers between devices  22.1 us (29%)
    ppermute x21, starting transfers between devices, flip(): return lax.ppermute(x, axis, [(i, i ^ k) for i in range(n)])  25.4 us
    pallas_call x7, Pallas kernels, partials(): pl.pallas_call(functools.partial(partials_kernel, count, groups, opening,...  25.3 us
    ppermute x21, waiting for transfers between devices, flip(): return lax.ppermute(x, axis, [(i, i ^ k) for i in range(n)])  22.1 us
    pallas_call x7, Pallas kernels, project(): pl.pallas_call(functools.partial(project_kernel, len(addends), pieces, fi...  2.12 us
    pallas_call x1, Pallas kernels, score(): pl.pallas_call(functools.partial(score_kernel, count), out_shape=jax.Shap...  1.72 us
  transfers between devices with their start and end apart: 21, of which 13 were waited for; matrix products, arithmetic and copies ran while one was open for 0% of the time, Pallas kernels for 29%

profile of v4, /device:TPU:0, one launch (start us, length us, event | category | flops | bytes accessed | tf_op | source)
XLA Modules:
  0.0 77.3 jit_solution(1967839276032433717)
XLA Ops:
  0.0 4.4 %partials_0.1 = (bf16[128,1536]{1,0:T(8,128)(2,1)S(1)}, bf16[128,1536]{1,0:T(8,128)(2,1)S(1)}, bf16[256,2048]{1,0:T(8,128)(2,1)S(1)}, bf16[256,2048]{1,0:T(8,128)(2,1)S(1)}, bf16[2048,512]{1,0:T(8,128)(2,1)S(1)}) custom-call(s32[1]{0:T(128)} %bitcast.refs_0_.e_ref, bf16[256,2048]{1,0:T(8,128)(2,1)} %refs_1_.1, bf16[256,2048]{1,0:T(8,128)(2,1)} %refs_2_.7, ...), custom_call_target="tpu_custom_call" | custom-call | flops 1610612736 | bytes 7077888 | tf_op jit(solution)/shard_map/partials_0/pallas_call | solution.py:165
  4.4 3.0 %collective-permute-start.12 = (bf16[128,1536]{1,0:T(8,128)(2,1)S(1)}, bf16[128,1536]{1,0:T(8,128)(2,1)S(1)}, u32[]{:S(2)}, u32[]{:S(2)}) collective-permute-start(bf16[128,1536]{1,0:T(8,128)(2,1)S(1)} %get-tuple-element.30.refs_6_), channel_id=1, source_target_pairs={{0,1},{1,0},{2,3},{3,2},{4,5},{5,4},{6,7},{7,6},{8,9},{9,8},{10,11... | collective-permute-start | bytes 1179656 | tf_op jit(solution)/shard_map/ppermute | solution.py:347
  7.4 3.6 %partials_512.1 = (bf16[128,1536]{1,0:T(8,128)(2,1)S(1)}, bf16[128,1536]{1,0:T(8,128)(2,1)S(1)}, bf16[2048,512]{1,0:T(8,128)(2,1)S(1)}) custom-call(bf16[256,2048]{1,0:T(8,128)(2,1)S(1)} %get-tuple-element.27.refs_0_, bf16[256,2048]{1,0:T(8,128)(2,1)S(1)} %get-tuple-element.28.refs_1_, bf16[2048,3584]{1,0:T(8,128)(2,1)} %refs_2_.13, ...), custom_call_target="tpu_custom_call" | custom-call | flops 1610612736 | bytes 7077888 | tf_op jit(solution)/shard_map/partials_512/pallas_call | solution.py:165
  11.0 1.6 %collective-permute-start.10 = (bf16[128,1536]{1,0:T(8,128)(2,1)S(1)}, bf16[128,1536]{1,0:T(8,128)(2,1)S(1)}, u32[]{:S(2)}, u32[]{:S(2)}) collective-permute-start(bf16[128,1536]{1,0:T(8,128)(2,1)S(1)} %get-tuple-element.32.refs_6_), channel_id=1, source_target_pairs={{0,2},{1,3},{2,0},{3,1},{4,6},{5,7},{6,4},{7,5},{8,10},{9,11},{10,... | collective-permute-start | bytes 1179656 | tf_op jit(solution)/shard_map/ppermute | solution.py:347
  12.6 3.5 %partials_1024.1 = (bf16[128,1536]{1,0:T(8,128)(2,1)S(1)}, bf16[128,1536]{1,0:T(8,128)(2,1)S(1)}, bf16[2048,512]{1,0:T(8,128)(2,1)S(1)}) custom-call(bf16[256,2048]{1,0:T(8,128)(2,1)S(1)} %get-tuple-element.27.refs_0_, bf16[256,2048]{1,0:T(8,128)(2,1)S(1)} %get-tuple-element.28.refs_1_, bf16[2048,3584]{1,0:T(8,128)(2,1)} %refs_2_.13, ...), custom_call_target="tpu_custom_call" | custom-call | flops 1610612736 | bytes 7077888 | tf_op jit(solution)/shard_map/partials_1024/pallas_call | solution.py:165
  16.1 0.6 collective-permute-start.8
  16.7 3.5 %partials_1536.1 = (bf16[128,1536]{1,0:T(8,128)(2,1)S(1)}, bf16[128,1536]{1,0:T(8,128)(2,1)S(1)}, bf16[2048,512]{1,0:T(8,128)(2,1)S(1)}) custom-call(bf16[256,2048]{1,0:T(8,128)(2,1)S(1)} %get-tuple-element.27.refs_0_, bf16[256,2048]{1,0:T(8,128)(2,1)S(1)} %get-tuple-element.28.refs_1_, bf16[2048,3584]{1,0:T(8,128)(2,1)} %refs_2_.13, ...), custom_call_target="tpu_custom_call" | custom-call | flops 1610612736 | bytes 7077888 | tf_op jit(solution)/shard_map/partials_1536/pallas_call | solution.py:165
  20.3 0.1 collective-permute-start.6
  20.4 3.6 %partials_2048.1 = (bf16[128,1664]{1,0:T(8,128)(2,1)S(1)}, bf16[128,1664]{1,0:T(8,128)(2,1)S(1)}, bf16[2048,512]{1,0:T(8,128)(2,1)S(1)}) custom-call(bf16[256,2048]{1,0:T(8,128)(2,1)S(1)} %get-tuple-element.27.refs_0_, bf16[256,2048]{1,0:T(8,128)(2,1)S(1)} %get-tuple-element.28.refs_1_, bf16[2048,3584]{1,0:T(8,128)(2,1)} %refs_2_.13, ...), custom_call_target="tpu_custom_call" | custom-call | flops 1744830464 | bytes 7143424 | tf_op jit(solution)/shard_map/partials_2048/pallas_call | solution.py:165
  24.0 2.0 %collective-permute-start.4 = (bf16[128,1664]{1,0:T(8,128)(2,1)S(1)}, bf16[128,1664]{1,0:T(8,128)(2,1)S(1)}, u32[]{:S(2)}, u32[]{:S(2)}) collective-permute-start(bf16[128,1664]{1,0:T(8,128)(2,1)S(1)} %get-tuple-element.38.refs_6_), channel_id=1, source_target_pairs={{0,1},{1,0},{2,3},{3,2},{4,5},{5,4},{6,7},{7,6},{8,9},{9,8},{10,11... | collective-permute-start | bytes 1277960 | tf_op jit(solution)/shard_map/ppermute | solution.py:347
  26.0 3.5 %partials_2560.1 = (bf16[128,1536]{1,0:T(8,128)(2,1)S(1)}, bf16[128,1536]{1,0:T(8,128)(2,1)S(1)}, bf16[2048,512]{1,0:T(8,128)(2,1)S(1)}) custom-call(bf16[256,2048]{1,0:T(8,128)(2,1)S(1)} %get-tuple-element.27.refs_0_, bf16[256,2048]{1,0:T(8,128)(2,1)S(1)} %get-tuple-element.28.refs_1_, bf16[2048,3584]{1,0:T(8,128)(2,1)} %refs_2_.13, ...), custom_call_target="tpu_custom_call" | custom-call | flops 1610612736 | bytes 7077888 | tf_op jit(solution)/shard_map/partials_2560/pallas_call | solution.py:165
  29.6 3.1 %partials_3072.1 = (bf16[128,1536]{1,0:T(8,128)(2,1)S(1)}, bf16[128,1536]{1,0:T(8,128)(2,1)S(1)}) custom-call(bf16[256,2048]{1,0:T(8,128)(2,1)S(1)} %get-tuple-element.27.refs_0_, bf16[256,2048]{1,0:T(8,128)(2,1)S(1)} %get-tuple-element.28.refs_1_, bf16[2048,3584]{1,0:T(8,128)(2,1)} %refs_2_.13, bf16[2048,3584]{1,0:T(8,128)(2,1)} %refs_3_.13, ...), custom_call_target="tpu_custom_call" | custom-call | flops 1610612736 | bytes 7077888 | tf_op jit(solution)/shard_map/partials_3072/pallas_call | solution.py:165
  32.7 1.6 %collective-permute-start.2 = (bf16[128,1536]{1,0:T(8,128)(2,1)S(1)}, bf16[128,1536]{1,0:T(8,128)(2,1)S(1)}, u32[]{:S(2)}, u32[]{:S(2)}) collective-permute-start(bf16[128,1536]{1,0:T(8,128)(2,1)S(1)} %get-tuple-element.40.refs_6_), channel_id=1, source_target_pairs={{0,2},{1,3},{2,0},{3,1},{4,6},{5,7},{6,4},{7,5},{8,10},{9,11},{10,... | collective-permute-start | bytes 1179656 | tf_op jit(solution)/shard_map/ppermute | solution.py:347
  34.3 0.6 collective-permute-start
  35.0 0.1 collective-permute-start.13
  35.1 2.0 %collective-permute-start.11 = (bf16[64,1536]{1,0:T(8,128)(2,1)S(1)}, bf16[64,1536]{1,0:T(8,128)(2,1)S(1)}, u32[]{:S(2)}, u32[]{:S(2)}) collective-permute-start(bf16[64,1536]{1,0:T(8,128)(2,1)S(1)} %add_convert_fusion.2), channel_id=1, source_target_pairs={{0,1},{1,0},{2,3},{3,2},{4,5},{5,4},{6,7},{7,6},{8,9},{9,8},{10,11... | collective-permute-start | bytes 589832 | tf_op jit(solution)/shard_map/ppermute | solution.py:347
  37.2 7.6 %collective-permute-done.2.refs_1_ = bf16[128,1536]{1,0:T(8,128)(2,1)S(1)} collective-permute-done((bf16[128,1536]{1,0:T(8,128)(2,1)S(1)}, bf16[128,1536]{1,0:T(8,128)(2,1)S(1)}, u32[]{:S(2)}, u32[]{:S(2)}) %collective-permute-start.2) | collective-permute-done | bytes 393248 | tf_op jit(solution)/shard_map/ppermute | solution.py:347
  44.8 1.5 %collective-permute-start.9 = (bf16[64,1536]{1,0:T(8,128)(2,1)S(1)}, bf16[64,1536]{1,0:T(8,128)(2,1)S(1)}, u32[]{:S(2)}, u32[]{:S(2)}) collective-permute-start(bf16[64,1536]{1,0:T(8,128)(2,1)S(1)} %add_convert_fusion.3), channel_id=1, source_target_pairs={{0,2},{1,3},{2,0},{3,1},{4,6},{5,7},{6,4},{7,5},{8,10},{9,11},{10,... | collective-permute-start | bytes 589832 | tf_op jit(solution)/shard_map/ppermute | solution.py:347
  46.4 0.6 collective-permute-start.7
  47.0 1.6 %collective-permute-start.3 = (bf16[64,1536]{1,0:T(8,128)(2,1)S(1)}, bf16[64,1536]{1,0:T(8,128)(2,1)S(1)}, u32[]{:S(2)}, u32[]{:S(2)}) collective-permute-start(bf16[64,1536]{1,0:T(8,128)(2,1)S(1)} %add_convert_fusion.5), channel_id=1, source_target_pairs={{0,1},{1,0},{2,3},{3,2},{4,5},{5,4},{6,7},{7,6},{8,9},{9,8},{10,11... | collective-permute-start | bytes 589832 | tf_op jit(solution)/shard_map/ppermute | solution.py:347
  48.6 0.4 collective-permute-done.13.refs_2_
  49.0 1.5 %collective-permute-start.5 = (bf16[64,1664]{1,0:T(8,128)(2,1)S(1)}, bf16[64,1664]{1,0:T(8,128)(2,1)S(1)}, u32[]{:S(2)}, u32[]{:S(2)}) collective-permute-start(bf16[64,1664]{1,0:T(8,128)(2,1)S(1)} %add_convert_fusion), channel_id=1, source_target_pairs={{0,2},{1,3},{2,0},{3,1},{4,6},{5,7},{6,4},{7,5},{8,10},{9,11},{10,... | collective-permute-start | bytes 638984 | tf_op jit(solution)/shard_map/ppermute | solution.py:347
  50.6 0.1 collective-permute-done.11.refs_2_
  50.6 0.5 collective-permute-start.1
  51.2 0.3 project_0.1.refs_6_
  51.4 0.3 project_512.1.refs_6_
  51.7 1.5 %collective-permute-done.9.refs_2_ = bf16[64,1536]{1,0:T(8,128)(2,1)S(1)} collective-permute-done((bf16[64,1536]{1,0:T(8,128)(2,1)S(1)}, bf16[64,1536]{1,0:T(8,128)(2,1)S(1)}, u32[]{:S(2)}, u32[]{:S(2)}) %collective-permute-start.9) | collective-permute-done | bytes 196640 | tf_op jit(solution)/shard_map/ppermute | solution.py:347
  53.2 0.3 project_1024.1.refs_6_
  53.5 1.1 %collective-permute-done.7.refs_2_ = bf16[64,1536]{1,0:T(8,128)(2,1)S(1)} collective-permute-done((bf16[64,1536]{1,0:T(8,128)(2,1)S(1)}, bf16[64,1536]{1,0:T(8,128)(2,1)S(1)}, u32[]{:S(2)}, u32[]{:S(2)}) %collective-permute-start.7) | collective-permute-done | bytes 196640 | tf_op jit(solution)/shard_map/ppermute | solution.py:347
  54.6 0.3 project_1536.1.refs_6_
  54.8 2.5 %collective-permute-done.5.refs_2_.refs_9_ = bf16[64,1664]{1,0:T(8,128)(2,1)S(1)} collective-permute-done((bf16[64,1664]{1,0:T(8,128)(2,1)S(1)}, bf16[64,1664]{1,0:T(8,128)(2,1)S(1)}, u32[]{:S(2)}, u32[]{:S(2)}) %collective-permute-start.5) | collective-permute-done | bytes 213024 | tf_op jit(solution)/shard_map/ppermute | solution.py:347
  57.3 0.3 project_2048.1.refs_6_
  57.5 0.3 project_2560.1.refs_6_
  57.8 1.6 %collective-permute-done.1.refs_2_ = bf16[64,1536]{1,0:T(8,128)(2,1)S(1)} collective-permute-done((bf16[64,1536]{1,0:T(8,128)(2,1)S(1)}, bf16[64,1536]{1,0:T(8,128)(2,1)S(1)}, u32[]{:S(2)}, u32[]{:S(2)}) %collective-permute-start.1) | collective-permute-done | bytes 196640 | tf_op jit(solution)/shard_map/ppermute | solution.py:347
  59.4 0.6 project_3072.1
  60.0 0.1 collective-permute-start.14
  60.0 1.2 %collective-permute-done.14 = bf16[96,128]{1,0:T(8,128)(2,1)S(1)} collective-permute-done((bf16[96,128]{1,0:T(8,128)(2,1)S(1)}, bf16[96,128]{1,0:T(8,128)(2,1)S(1)}, u32[]{:S(2)}, u32[]{:S(2)}) %collective-permute-start.14) | collective-permute-done | bytes 24608 | tf_op jit(solution)/shard_map/ppermute | solution.py:347
  61.2 3.7 %collective-permute-start.17 = (bf16[96,128]{1,0:T(8,128)(2,1)S(1)}, bf16[96,128]{1,0:T(8,128)(2,1)S(1)}, u32[]{:S(2)}, u32[]{:S(2)}) collective-permute-start(bf16[96,128]{1,0:T(8,128)(2,1)S(1)} %add_convert_fusion.8), channel_id=1, source_target_pairs={{0,24},{4,28},{8,16},{12,20},{16,8},{20,12},{24,0},{28,4},{1,25},{... | collective-permute-start | bytes 73736 | tf_op jit(solution)/shard_map/ppermute | solution.py:347
  64.9 0.8 %collective-permute-start.15 = (bf16[96,128]{1,0:T(8,128)(2,1)S(1)}, bf16[96,128]{1,0:T(8,128)(2,1)S(1)}, u32[]{:S(2)}, u32[]{:S(2)}) collective-permute-start(bf16[96,128]{1,0:T(8,128)(2,1)S(1)} %add_convert_fusion.8), channel_id=1, source_target_pairs={{0,8},{4,12},{8,0},{12,4},{16,24},{20,28},{24,16},{28,20},{1,9},{5... | collective-permute-start | bytes 73736 | tf_op jit(solution)/shard_map/ppermute | solution.py:347
  65.7 1.2 %collective-permute-done.17 = bf16[96,128]{1,0:T(8,128)(2,1)S(1)} collective-permute-done((bf16[96,128]{1,0:T(8,128)(2,1)S(1)}, bf16[96,128]{1,0:T(8,128)(2,1)S(1)}, u32[]{:S(2)}, u32[]{:S(2)}) %collective-permute-start.17) | collective-permute-done | bytes 24608 | tf_op jit(solution)/shard_map/ppermute | solution.py:347
  66.9 2.7 %collective-permute-done.16 = bf16[96,128]{1,0:T(8,128)(2,1)S(1)} collective-permute-done((bf16[96,128]{1,0:T(8,128)(2,1)S(1)}, bf16[96,128]{1,0:T(8,128)(2,1)S(1)}, u32[]{:S(2)}, u32[]{:S(2)}) %collective-permute-start.16) | collective-permute-done | bytes 24608 | tf_op jit(solution)/shard_map/ppermute | solution.py:347
  69.7 1.6 %collective-permute-start.20 = (bf16[96,128]{1,0:T(8,128)(2,1)S(1)}, bf16[96,128]{1,0:T(8,128)(2,1)S(1)}, u32[]{:S(2)}, u32[]{:S(2)}) collective-permute-start(bf16[96,128]{1,0:T(8,128)(2,1)S(1)} %add_convert_fusion.7.refs_0_), channel_id=1, source_target_pairs={{0,3},{1,2},{2,1},{3,0},{4,7},{5,6},{6,5},{7,4},{8,11},{9,10},{10,... | collective-permute-start | bytes 73736 | tf_op jit(solution)/shard_map/ppermute | solution.py:347
  71.2 0.5 collective-permute-start.19
  71.7 1.5 %collective-permute-start.18 = (bf16[96,128]{1,0:T(8,128)(2,1)S(1)}, bf16[96,128]{1,0:T(8,128)(2,1)S(1)}, u32[]{:S(2)}, u32[]{:S(2)}) collective-permute-start(bf16[96,128]{1,0:T(8,128)(2,1)S(1)} %add_convert_fusion.7.refs_0_), channel_id=1, source_target_pairs={{0,1},{1,0},{2,3},{3,2},{4,5},{5,4},{6,7},{7,6},{8,9},{9,8},{10,11... | collective-permute-start | bytes 73736 | tf_op jit(solution)/shard_map/ppermute | solution.py:347
  73.2 1.2 %collective-permute-done.20.refs_3_ = bf16[96,128]{1,0:T(8,128)(2,1)S(1)} collective-permute-done((bf16[96,128]{1,0:T(8,128)(2,1)S(1)}, bf16[96,128]{1,0:T(8,128)(2,1)S(1)}, u32[]{:S(2)}, u32[]{:S(2)}) %collective-permute-start.20) | collective-permute-done | bytes 24608 | tf_op jit(solution)/shard_map/ppermute | solution.py:347
  74.5 0.6 collective-permute-done.19.refs_2_
  75.0 0.5 collective-permute-done.18.refs_1_
  75.6 1.7 %score.1 = f32[4,128]{1,0:T(4,128)} custom-call(s32[1]{0:T(128)} %bitcast.refs_0_.e_ref, bf16[96,128]{1,0:T(8,128)(2,1)S(1)} %add_convert_fusion.7.refs_0_, bf16[96,128]{1,0:T(8,128)(2,1)S(1)} %collective-permute-done.18.refs_1_, bf16[96,128]{1,0:T(8,128)(2,1)S(1)} %collective-permute-done.19.refs_2_, bf16[96,128]{1,0:T(8,128)(2,1)S(1)} %collective-permute-done.20.refs_3_, ...), custom_call_target="tpu_custom_call" | custom-call | tf_op jit(solution)/shard_map/score/pallas_call | solution.py:313
  (33 shorter events, 0.4 us)
Async XLA Ops:
  4.4 28.2 %collective-permute-start.12 = (bf16[128,1536]{1,0:T(8,128)(2,1)S(1)}, bf16[128,1536]{1,0:T(8,128)(2,1)S(1)}, u32[]{:S(2)}, u32[]{:S(2)}) collective-permute-start(bf16[128,1536]{1,0:T(8,128)(2,1)S(1)} %get-tuple-element.30.refs_6_), channel_id=1, source_target_pairs={{0,1},{1,0},{2,3},{3,2},{4,5},{5,4},{6,7},{7,6},{8,9},{9,8},{10,11... | collective-permute-start | bytes 1179656 | tf_op jit(solution)/shard_map/ppermute | solution.py:347
  11.0 23.3 %collective-permute-start.10 = (bf16[128,1536]{1,0:T(8,128)(2,1)S(1)}, bf16[128,1536]{1,0:T(8,128)(2,1)S(1)}, u32[]{:S(2)}, u32[]{:S(2)}) collective-permute-start(bf16[128,1536]{1,0:T(8,128)(2,1)S(1)} %get-tuple-element.32.refs_6_), channel_id=1, source_target_pairs={{0,2},{1,3},{2,0},{3,1},{4,6},{5,7},{6,4},{7,5},{8,10},{9,11},{10,... | collective-permute-start | bytes 1179656 | tf_op jit(solution)/shard_map/ppermute | solution.py:347
  16.1 18.9 %collective-permute-start.8 = (bf16[128,1536]{1,0:T(8,128)(2,1)S(1)}, bf16[128,1536]{1,0:T(8,128)(2,1)S(1)}, u32[]{:S(2)}, u32[]{:S(2)}) collective-permute-start(bf16[128,1536]{1,0:T(8,128)(2,1)S(1)} %get-tuple-element.34.refs_6_), channel_id=1, source_target_pairs={{0,1},{1,0},{2,3},{3,2},{4,5},{5,4},{6,7},{7,6},{8,9},{9,8},{10,11... | collective-permute-start | bytes 1179656 | tf_op jit(solution)/shard_map/ppermute | solution.py:347
  16.7 3.6 %copy-start.4 = (bf16[2048,64]{0,1:T(8,128)(2,1)S(1)}, bf16[2048,64]{0,1:T(8,128)(2,1)}, u32[]{:S(2)}) copy-start(bf16[2048,64]{0,1:T(8,128)(2,1)} %param.17) | copy-start | bytes 786436
  16.7 3.6 %copy-start.5 = (bf16[2048,64]{0,1:T(8,128)(2,1)S(1)}, bf16[2048,64]{0,1:T(8,128)(2,1)}, u32[]{:S(2)}) copy-start(bf16[2048,64]{0,1:T(8,128)(2,1)} %param.21) | copy-start | bytes 786436
  20.3 14.9 %collective-permute-start.6 = (bf16[128,1536]{1,0:T(8,128)(2,1)S(1)}, bf16[128,1536]{1,0:T(8,128)(2,1)S(1)}, u32[]{:S(2)}, u32[]{:S(2)}) collective-permute-start(bf16[128,1536]{1,0:T(8,128)(2,1)S(1)} %get-tuple-element.36.refs_8_), channel_id=1, source_target_pairs={{0,2},{1,3},{2,0},{3,1},{4,6},{5,7},{6,4},{7,5},{8,10},{9,11},{10,... | collective-permute-start | bytes 1179656 | tf_op jit(solution)/shard_map/ppermute | solution.py:347
  24.0 22.4 %collective-permute-start.4 = (bf16[128,1664]{1,0:T(8,128)(2,1)S(1)}, bf16[128,1664]{1,0:T(8,128)(2,1)S(1)}, u32[]{:S(2)}, u32[]{:S(2)}) collective-permute-start(bf16[128,1664]{1,0:T(8,128)(2,1)S(1)} %get-tuple-element.38.refs_6_), channel_id=1, source_target_pairs={{0,1},{1,0},{2,3},{3,2},{4,5},{5,4},{6,7},{7,6},{8,9},{9,8},{10,11... | collective-permute-start | bytes 1277960 | tf_op jit(solution)/shard_map/ppermute | solution.py:347
  32.7 12.1 %collective-permute-start.2 = (bf16[128,1536]{1,0:T(8,128)(2,1)S(1)}, bf16[128,1536]{1,0:T(8,128)(2,1)S(1)}, u32[]{:S(2)}, u32[]{:S(2)}) collective-permute-start(bf16[128,1536]{1,0:T(8,128)(2,1)S(1)} %get-tuple-element.40.refs_6_), channel_id=1, source_target_pairs={{0,2},{1,3},{2,0},{3,1},{4,6},{5,7},{6,4},{7,5},{8,10},{9,11},{10,... | collective-permute-start | bytes 1179656 | tf_op jit(solution)/shard_map/ppermute | solution.py:347
  34.2 16.9 %copy-start = (bf16[3584,64]{0,1:T(8,128)(2,1)S(1)}, bf16[3584,64]{0,1:T(8,128)(2,1)}, u32[]{:S(2)}) copy-start(bf16[3584,64]{0,1:T(8,128)(2,1)} %param.18) | copy-start | bytes 1376260
  34.2 16.9 %copy-start.1 = (bf16[3584,64]{0,1:T(8,128)(2,1)S(1)}, bf16[3584,64]{0,1:T(8,128)(2,1)}, u32[]{:S(2)}) copy-start(bf16[3584,64]{0,1:T(8,128)(2,1)} %param.19) | copy-start | bytes 1376260
  34.2 16.9 %copy-start.2 = (bf16[3584,64]{0,1:T(8,128)(2,1)S(1)}, bf16[3584,64]{0,1:T(8,128)(2,1)}, u32[]{:S(2)}) copy-start(bf16[3584,64]{0,1:T(8,128)(2,1)} %param.20) | copy-start | bytes 1376260
  34.3 12.7 %collective-permute-start = (bf16[128,1536]{1,0:T(8,128)(2,1)S(1)}, bf16[128,1536]{1,0:T(8,128)(2,1)S(1)}, u32[]{:S(2)}, u32[]{:S(2)}) collective-permute-start(bf16[128,1536]{1,0:T(8,128)(2,1)S(1)} %get-tuple-element.42), channel_id=1, source_target_pairs={{0,1},{1,0},{2,3},{3,2},{4,5},{5,4},{6,7},{7,6},{8,9},{9,8},{10,11... | collective-permute-start | bytes 1179656 | tf_op jit(solution)/shard_map/ppermute | solution.py:347
  35.0 14.0 %collective-permute-start.13 = (bf16[64,1536]{1,0:T(8,128)(2,1)S(1)}, bf16[64,1536]{1,0:T(8,128)(2,1)S(1)}, u32[]{:S(2)}, u32[]{:S(2)}) collective-permute-start(bf16[64,1536]{1,0:T(8,128)(2,1)S(1)} %add_convert_fusion.1), channel_id=1, source_target_pairs={{0,2},{1,3},{2,0},{3,1},{4,6},{5,7},{6,4},{7,5},{8,10},{9,11},{10,... | collective-permute-start | bytes 589832 | tf_op jit(solution)/shard_map/ppermute | solution.py:347
  35.1 15.5 %collective-permute-start.11 = (bf16[64,1536]{1,0:T(8,128)(2,1)S(1)}, bf16[64,1536]{1,0:T(8,128)(2,1)S(1)}, u32[]{:S(2)}, u32[]{:S(2)}) collective-permute-start(bf16[64,1536]{1,0:T(8,128)(2,1)S(1)} %add_convert_fusion.2), channel_id=1, source_target_pairs={{0,1},{1,0},{2,3},{3,2},{4,5},{5,4},{6,7},{7,6},{8,9},{9,8},{10,11... | collective-permute-start | bytes 589832 | tf_op jit(solution)/shard_map/ppermute | solution.py:347
  44.8 8.4 %collective-permute-start.9 = (bf16[64,1536]{1,0:T(8,128)(2,1)S(1)}, bf16[64,1536]{1,0:T(8,128)(2,1)S(1)}, u32[]{:S(2)}, u32[]{:S(2)}) collective-permute-start(bf16[64,1536]{1,0:T(8,128)(2,1)S(1)} %add_convert_fusion.3), channel_id=1, source_target_pairs={{0,2},{1,3},{2,0},{3,1},{4,6},{5,7},{6,4},{7,5},{8,10},{9,11},{10,... | collective-permute-start | bytes 589832 | tf_op jit(solution)/shard_map/ppermute | solution.py:347
  46.4 8.2 %collective-permute-start.7 = (bf16[64,1536]{1,0:T(8,128)(2,1)S(1)}, bf16[64,1536]{1,0:T(8,128)(2,1)S(1)}, u32[]{:S(2)}, u32[]{:S(2)}) collective-permute-start(bf16[64,1536]{1,0:T(8,128)(2,1)S(1)} %add_convert_fusion.4), channel_id=1, source_target_pairs={{0,1},{1,0},{2,3},{3,2},{4,5},{5,4},{6,7},{7,6},{8,9},{9,8},{10,11... | collective-permute-start | bytes 589832 | tf_op jit(solution)/shard_map/ppermute | solution.py:347
  47.0 10.5 %collective-permute-start.3 = (bf16[64,1536]{1,0:T(8,128)(2,1)S(1)}, bf16[64,1536]{1,0:T(8,128)(2,1)S(1)}, u32[]{:S(2)}, u32[]{:S(2)}) collective-permute-start(bf16[64,1536]{1,0:T(8,128)(2,1)S(1)} %add_convert_fusion.5), channel_id=1, source_target_pairs={{0,1},{1,0},{2,3},{3,2},{4,5},{5,4},{6,7},{7,6},{8,9},{9,8},{10,11... | collective-permute-start | bytes 589832 | tf_op jit(solution)/shard_map/ppermute | solution.py:347
  49.0 8.3 %collective-permute-start.5 = (bf16[64,1664]{1,0:T(8,128)(2,1)S(1)}, bf16[64,1664]{1,0:T(8,128)(2,1)S(1)}, u32[]{:S(2)}, u32[]{:S(2)}) collective-permute-start(bf16[64,1664]{1,0:T(8,128)(2,1)S(1)} %add_convert_fusion), channel_id=1, source_target_pairs={{0,2},{1,3},{2,0},{3,1},{4,6},{5,7},{6,4},{7,5},{8,10},{9,11},{10,... | collective-permute-start | bytes 638984 | tf_op jit(solution)/shard_map/ppermute | solution.py:347
  50.6 8.7 %collective-permute-start.1 = (bf16[64,1536]{1,0:T(8,128)(2,1)S(1)}, bf16[64,1536]{1,0:T(8,128)(2,1)S(1)}, u32[]{:S(2)}, u32[]{:S(2)}) collective-permute-start(bf16[64,1536]{1,0:T(8,128)(2,1)S(1)} %add_convert_fusion.6), channel_id=1, source_target_pairs={{0,2},{1,3},{2,0},{3,1},{4,6},{5,7},{6,4},{7,5},{8,10},{9,11},{10,... | collective-permute-start | bytes 589832 | tf_op jit(solution)/shard_map/ppermute | solution.py:347
  57.8 17.8 %copy-start.3 = (bf16[128,12288]{1,0:T(8,128)(2,1)S(1)}, bf16[128,12288]{1,0:T(8,128)(2,1)}, u32[]{:S(2)}) copy-start(bf16[128,12288]{1,0:T(8,128)(2,1)} %refs_4_.15) | copy-start | bytes 9437188
  57.8 17.7 %copy-start.6 = (s32[1,128]{1,0:T(1,128)S(1)}, s32[1,128]{1,0:T(1,128)}, u32[]{:S(2)}) copy-start(s32[1,128]{1,0:T(1,128)} %refs_5_.3) | copy-start | bytes 1540
  60.0 1.3 %collective-permute-start.14 = (bf16[96,128]{1,0:T(8,128)(2,1)S(1)}, bf16[96,128]{1,0:T(8,128)(2,1)S(1)}, u32[]{:S(2)}, u32[]{:S(2)}) collective-permute-start(bf16[96,128]{1,0:T(8,128)(2,1)S(1)} %project_3072.1), channel_id=1, source_target_pairs={{0,4},{4,0},{8,12},{12,8},{16,20},{20,16},{24,28},{28,24},{1,5},{5... | collective-permute-start | bytes 73736 | tf_op jit(solution)/shard_map/ppermute | solution.py:347
  61.2 5.7 %collective-permute-start.17 = (bf16[96,128]{1,0:T(8,128)(2,1)S(1)}, bf16[96,128]{1,0:T(8,128)(2,1)S(1)}, u32[]{:S(2)}, u32[]{:S(2)}) collective-permute-start(bf16[96,128]{1,0:T(8,128)(2,1)S(1)} %add_convert_fusion.8), channel_id=1, source_target_pairs={{0,24},{4,28},{8,16},{12,20},{16,8},{20,12},{24,0},{28,4},{1,25},{... | collective-permute-start | bytes 73736 | tf_op jit(solution)/shard_map/ppermute | solution.py:347
  64.9 4.7 %collective-permute-start.16 = (bf16[96,128]{1,0:T(8,128)(2,1)S(1)}, bf16[96,128]{1,0:T(8,128)(2,1)S(1)}, u32[]{:S(2)}, u32[]{:S(2)}) collective-permute-start(bf16[96,128]{1,0:T(8,128)(2,1)S(1)} %add_convert_fusion.8), channel_id=1, source_target_pairs={{0,16},{4,20},{8,24},{12,28},{16,0},{20,4},{24,8},{28,12},{1,17},{... | collective-permute-start | bytes 73736 | tf_op jit(solution)/shard_map/ppermute | solution.py:347
  64.9 4.7 %collective-permute-start.15 = (bf16[96,128]{1,0:T(8,128)(2,1)S(1)}, bf16[96,128]{1,0:T(8,128)(2,1)S(1)}, u32[]{:S(2)}, u32[]{:S(2)}) collective-permute-start(bf16[96,128]{1,0:T(8,128)(2,1)S(1)} %add_convert_fusion.8), channel_id=1, source_target_pairs={{0,8},{4,12},{8,0},{12,4},{16,24},{20,28},{24,16},{28,20},{1,9},{5... | collective-permute-start | bytes 73736 | tf_op jit(solution)/shard_map/ppermute | solution.py:347
  69.7 4.8 %collective-permute-start.20 = (bf16[96,128]{1,0:T(8,128)(2,1)S(1)}, bf16[96,128]{1,0:T(8,128)(2,1)S(1)}, u32[]{:S(2)}, u32[]{:S(2)}) collective-permute-start(bf16[96,128]{1,0:T(8,128)(2,1)S(1)} %add_convert_fusion.7.refs_0_), channel_id=1, source_target_pairs={{0,3},{1,2},{2,1},{3,0},{4,7},{5,6},{6,5},{7,4},{8,11},{9,10},{10,... | collective-permute-start | bytes 73736 | tf_op jit(solution)/shard_map/ppermute | solution.py:347
  71.2 3.8 %collective-permute-start.19 = (bf16[96,128]{1,0:T(8,128)(2,1)S(1)}, bf16[96,128]{1,0:T(8,128)(2,1)S(1)}, u32[]{:S(2)}, u32[]{:S(2)}) collective-permute-start(bf16[96,128]{1,0:T(8,128)(2,1)S(1)} %add_convert_fusion.7.refs_0_), channel_id=1, source_target_pairs={{0,2},{1,3},{2,0},{3,1},{4,6},{5,7},{6,4},{7,5},{8,10},{9,11},{10,... | collective-permute-start | bytes 73736 | tf_op jit(solution)/shard_map/ppermute | solution.py:347
  71.7 3.8 %collective-permute-start.18 = (bf16[96,128]{1,0:T(8,128)(2,1)S(1)}, bf16[96,128]{1,0:T(8,128)(2,1)S(1)}, u32[]{:S(2)}, u32[]{:S(2)}) collective-permute-start(bf16[96,128]{1,0:T(8,128)(2,1)S(1)} %add_convert_fusion.7.refs_0_), channel_id=1, source_target_pairs={{0,1},{1,0},{2,3},{3,2},{4,5},{5,4},{6,7},{7,6},{8,9},{9,8},{10,11... | collective-permute-start | bytes 73736 | tf_op jit(solution)/shard_map/ppermute | solution.py:347
